TPU v7x, 512 devices: a whole 4x8x8 slice. The times are simulated.
512 devices in a mesh: row: 32 (over y_lo, x, core), col: 16 (over z, y_hi).
Axes of the slice: x: 4, y: 8 (y_hi: 2, y_lo: 4; y = y_hi * 4 + y_lo), z: 8, core: 2. Of those that a mesh axis runs over, the one named last changes fastest.
Arguments:
- telemetry: int32 [65536, 64], P(('col', 'row')), may hold values from -127 to 127
- scales: int32 [65536], P(('col', 'row')), may hold values from 1 to 4
- bands: int32 [32, 32], replicated, may hold values from 256 to 4096
- noise: float32 [65536], P('row'), may hold values from 0.5 to 2
- start: bfloat16 [65536, 64], P(('col', 'row')), may hold values from -6 to 6
- target: bfloat16 [65536, 64], P('row'), may hold values from -6 to 6
Outputs:
- first: float32 [65536, 64], P('row')
- second: float32 [65536, 64], P('row')
All inputs are finite; a program needn't handle non-finite values.
Results may differ from a plain program's by a relative error of at most 0.0023.
Values may be sent and summed in bfloat16 or wider, within the bound.
A program may use at most 128 MiB of HBM per device.

v0:
```python
import math

import jax
import jax.numpy as jnp
from jax import lax
from jax.sharding import Mesh
from jax.sharding import PartitionSpec as P

SUBAP = 2048
COL = ("col_0", "col_1")
COL_ROW = ("col_0", "col_1", "row")


damping = 0.4


def laid_out(parts, dim):
    parts = jnp.moveaxis(parts, 0, dim)
    dims = parts.shape
    return parts.reshape(*dims[:dim], dims[dim] * dims[dim + 1], *dims[dim + 2 :])


def copy_for_each(array, axis):
    copies = jnp.broadcast_to(array, (lax.axis_size(axis), *array.shape))
    return lax.all_to_all(copies, axis, split_axis=0, concat_axis=0, tiled=True)


def collect(array, axis, dim):
    return laid_out(copy_for_each(array, axis), dim)


def broadcast_by_axis(array, axes, root):
    array = jnp.where(lax.axis_index(axes) == root, array, jnp.zeros_like(array))
    for axis in axes:
        array = lax.psum(array, axis)
    return array


def split_up(array, dim, count):
    dims = array.shape
    parts = array.reshape(*dims[:dim], count, dims[dim] // count, *dims[dim + 1 :])
    return jnp.moveaxis(parts, dim, 0)


def sent_and_summed(array, axis, dim):
    count = lax.axis_size(axis)
    parts = lax.all_to_all(split_up(array, dim, count), axis, 0, 0, tiled=True)
    return jnp.sum(parts, axis=0)


def broadcast(array, axis, root):
    return lax.dynamic_index_in_dim(lax.all_gather(array, axis), root, 0, keepdims=False)


def on_device(telemetry, scales, bands, noise, start, target):
    frame_count = telemetry.shape[1]
    row_count = lax.axis_size("row")
    col_count = lax.axis_size(COL)
    ratio = row_count // col_count
    row_id = lax.axis_index("row")
    col_id = lax.axis_index(COL)
    order_total = telemetry.shape[0] * row_count * col_count
    norm_count = jnp.float32(order_total // 4)
    slopes = (telemetry.astype(jnp.float32) * scales.astype(jnp.float32)[:, None] / 128.0).astype(
        jnp.bfloat16
    )
    joined = jnp.concatenate([slopes, start], axis=1)
    col_joined = collect(joined, "row", 0)
    col_width = col_joined.shape[0]
    row_height = col_width // ratio
    half = lax.dynamic_slice_in_dim(col_joined, row_id % ratio * row_height, row_height, 0)
    row_joined = broadcast_by_axis(half, COL, row_id // ratio)
    row_slopes = row_joined[:, :frame_count]
    row_start = row_joined[:, frame_count:]
    col_slopes = col_joined[:, :frame_count]
    col_start = col_joined[:, frame_count:]
    panel_width = col_start.shape[1]
    row_f = row_slopes.astype(jnp.float32)
    weight = damping / (jnp.sum(row_f * row_f, axis=1) / norm_count + noise)
    count = bands.shape[0]
    index = jnp.arange(count, dtype=jnp.int32)
    sym = jnp.where(index[:, None] <= index[None, :], bands, bands.T).astype(jnp.float32)
    row_ids = row_id * row_height + jnp.arange(row_height, dtype=jnp.int32)
    onehot = (row_ids[:, None] // SUBAP == index[None, :]).astype(jnp.float32)
    row_band = jnp.dot(onehot, sym, precision=lax.Precision.HIGHEST)
    row_pos = (row_ids % SUBAP).astype(jnp.float32)
    width = math.gcd(math.gcd(col_width, 512), SUBAP)
    nblocks = col_width // width

    def build(step, carry):
        tile, acc = carry
        offset = step * width
        cols = lax.dynamic_slice_in_dim(col_slopes, offset, width, 0)
        raw = (
            lax.dot_general(
                row_slopes, cols, (((1,), (1,)), ((), ())), preferred_element_type=jnp.float32
            )
            / norm_count
        )
        col_ids = col_id * col_width + offset + jnp.arange(width, dtype=jnp.int32)
        band = lax.dynamic_slice_in_dim(row_band, (col_id * col_width + offset) // SUBAP, 1, 1)
        dist = jnp.abs(row_pos[:, None] - (col_ids % SUBAP).astype(jnp.float32)[None, :])
        taper = jnp.maximum(0.0, 1.0 - dist / band)
        diag = jnp.where(row_ids[:, None] == col_ids[None, :], noise[:, None], jnp.float32(0.0))
        entry = (taper * raw + diag).astype(jnp.bfloat16)
        tile = lax.dynamic_update_slice_in_dim(tile, entry, offset, 1)
        return (tile, acc)

    tile_init = jnp.zeros((row_height, col_width), jnp.bfloat16)
    acc_init = jnp.zeros((row_height, panel_width), jnp.float32)
    tile, acc = lax.fori_loop(0, nblocks, build, (tile_init, acc_init))
    product0 = jnp.dot(tile, col_start, preferred_element_type=jnp.float32)
    target_f = target.astype(jnp.float32)

    def refine(current, product):
        share = sent_and_summed(product, COL, 0)
        share_rows = row_height // col_count
        begin = col_id * share_rows
        cur_part = lax.dynamic_slice_in_dim(current, begin, share_rows, 0)
        tgt_part = lax.dynamic_slice_in_dim(target_f, begin, share_rows, 0)
        wgt_part = lax.dynamic_slice_in_dim(weight, begin, share_rows, 0)
        updated = cur_part + wgt_part[:, None] * (tgt_part - share)
        return collect(updated, COL, 0)

    first = refine(row_start.astype(jnp.float32), product0)
    first_low = first.astype(jnp.bfloat16)
    pieces = [broadcast(first_low, "row", col_id * ratio + offset_q) for offset_q in range(ratio)]
    col_first = jnp.concatenate(pieces, axis=0)
    product1 = jnp.dot(tile, col_first, preferred_element_type=jnp.float32)
    second = refine(first, product1)
    return (first, second)


def solution(mesh):
    finer = Mesh(mesh.devices.reshape(mesh.shape["row"], 8, 2), ("row", "col_0", "col_1"))
    placed = (P(COL_ROW, None), P(COL_ROW), P(), P("row"), P(COL_ROW, None), P("row", None))
    return jax.shard_map(
        on_device,
        mesh=finer,
        in_specs=placed,
        out_specs=(P("row", None), P("row", None)),
        check_vma=False,
    )
```

profile of v0, /device:TPU:10, one launch (start us, length us, event | category | flops | bytes accessed | tf_op | source)
XLA Modules:
  0.0 425.8 jit_solution(2020574549629206897)
XLA Ops:
  7.2 0.7 convert_element_type.63
  7.8 0.8 multiply_convert_fusion
  8.6 0.7 pad_maximum_fusion
  9.3 1.2 broadcast_in_dim.58
  10.5 0.0 copy-start.2
  10.5 9.5 %all-to-all-start = ((bf16[32,128,128]{1,2,0:T(8,128)(2,1)}), bf16[32,128,128]{1,2,0:T(8,128)(2,1)S(1)}, u32[]{:S(2)}, u32[]{:S(2)}) async-start(bf16[32,128,128]{1,2,0:T(8,128)(2,1)} %broadcast_in_dim.58), calls=%async_computation | async-start | bytes 2097152 | tf_op jit(solution)/shard_map/all_to_all | solution.py:25
  20.1 0.0 all-reduce.3.cloned.1.call-start
  20.1 24.6 %all-to-all-done = bf16[32,128,128]{1,2,0:T(8,128)(2,1)S(1)} async-done(((bf16[32,128,128]{1,2,0:T(8,128)(2,1)}), bf16[32,128,128]{1,2,0:T(8,128)(2,1)S(1)}, u32[]{:S(2)}, u32[]{:S(2)}) %all-to-all-start) | async-done | bytes 1048608 | tf_op jit(solution)/shard_map/all_to_all | solution.py:25
  44.8 0.7 copy.31
  45.5 0.2 copy.40
  45.7 0.8 broadcast_select_fusion
  46.5 0.0 all-reduce.3.cloned.1.call-update
  46.5 0.0 all-reduce.5.cloned.1.call-start
  46.6 81.7 %all-reduce.3.cloned.1.call-done = bf16[2048,128]{0,1:T(8,128)(2,1)} async-done(((bf16[2048,128]{0,1:T(8,128)(2,1)}), bf16[2048,128]{0,1:T(8,128)(2,1)}) %all-reduce.3.cloned.1.call-update) | async-done | bytes 524304 | tf_op jit(solution)/shard_map/psum | solution.py:35
  128.3 0.0 all-reduce.5.cloned.1.call-update
  128.3 0.0 copy-done.2
  128.3 0.1 copy.33
  128.4 0.8 fusion.14
  129.3 59.7 %all-reduce.5.cloned.1.call-done = bf16[2048,128]{0,1:T(8,128)(2,1)} async-done(((bf16[2048,128]{0,1:T(8,128)(2,1)}), bf16[2048,128]{0,1:T(8,128)(2,1)}) %all-reduce.5.cloned.1.call-update) | async-done | bytes 524304 | tf_op jit(solution)/shard_map/psum | solution.py:35
  189.0 1.1 fusion.30
  190.0 0.3 copy.34
  190.3 0.0 copy-start.3
  190.3 6.0 %broadcast_in_dim.60 = bf16[2048,4096]{0,1:T(8,128)(2,1)} broadcast(bf16[]{:T(256)} %constant.210.clone.1), dimensions={} | broadcast | bytes 16777218 | tf_op jit(solution)/shard_map/broadcast_in_dim | solution.py:109
  196.3 0.0 copy-done.3
  196.3 23.1 %while.17 = (s32[]{:T(128)}, bf16[2048,4096]{0,1:T(8,128)(2,1)}, s32[]{:T(128)}, f32[2048,32]{0,1:T(8,128)S(1)}, bf16[4096,64]{1,0:T(8,128)(2,1)S(1)}, /*index=5...) while((s32[]{:T(128)}, bf16[2048,4096]{0,1:T(8,128)(2,1)}, ...), condition=%wide.region_4.5_spmd.clone.clone, body=%wide.region_3.4_spmd.clone.clone.sunk | while | flops 145785376 | bytes 2827667 | solution.py:111
  196.4 2.9 fusion.45
  199.3 2.8 fusion.45
  202.2 2.8 fusion.45
  205.1 2.9 fusion.45
  208.0 2.8 fusion.45
  210.9 2.8 fusion.45
  213.8 2.8 fusion.45
  216.7 2.8 fusion.45
  219.5 0.0 copy-start
  219.5 9.0 %convolution_bitcast_fusion.1 = f32[8,16,8,128]{3,2,1,0:T(8,128)S(1)} fusion(bf16[2048,4096]{0,1:T(8,128)(2,1)} %get-tuple-element.227, bf16[4096,128]{1,0:T(8,128)(2,1)S(1)} %bitcast.53), kind=kOutput, calls=%fused_computation.22 | convolution fusion | flops 1073741824 | bytes 18350080 | tf_op jit(solution)/shard_map/dot_general | solution.py:112
  228.4 0.8 copy.50
  229.3 8.3 %all-to-all-start.1 = ((f32[16,128,64]{1,2,0:T(8,128)}), f32[16,128,64]{1,2,0:T(8,128)S(1)}, u32[]{:S(2)}, u32[]{:S(2)}) async-start(f32[16,128,64]{1,2,0:T(8,128)} %bitcast.43), calls=%async_computation.1 | async-start | bytes 1048576 | tf_op jit(solution)/shard_map/all_to_all | solution.py:47
  237.6 0.0 all-gather.2.cloned.1.call-start
  237.6 0.0 copy-done
  237.7 0.1 multiply_reduce_fusion
  237.7 0.1 fusion.28
  237.8 20.3 %all-to-all-done.1 = f32[16,128,64]{1,2,0:T(8,128)S(1)} async-done(((f32[16,128,64]{1,2,0:T(8,128)}), f32[16,128,64]{1,2,0:T(8,128)S(1)}, u32[]{:S(2)}, u32[]{:S(2)}) %all-to-all-start.1) | async-done | bytes 524320 | tf_op jit(solution)/shard_map/all_to_all | solution.py:47
  258.1 0.7 fusion.22
  258.9 24.4 %all_to_all.25 = f32[16,128,64]{1,2,0:T(8,128)S(1)} all-to-all(f32[16,128,64]{1,2,0:T(8,128)S(1)} %broadcast_in_dim.61), channel_id=1, replica_groups=mesh['row'=32,'col_0'=8,'col_1'=2] {'col_0','col_1'}, dimensions={0} | all-to-all | bytes 1048576 | tf_op jit(solution)/shard_map/all_to_all | solution.py:25
  283.3 0.2 copy.37
  283.5 0.8 convert_element_type.71
  284.3 0.0 all-gather.2.cloned.1.call-update
  284.4 65.9 %all-gather.2.cloned.1.call-done = bf16[32,2048,64]{1,2,0:T(8,128)(2,1)} async-done(((bf16[1,2048,64]{1,2,0:T(8,128)(2,1)}), bf16[32,2048,64]{1,2,0:T(8,128)(2,1)}) %all-gather.2.cloned.1.call-update) | async-done | bytes 8388624 | tf_op jit(solution)/shard_map/all_gather | solution.py:52
  350.3 1.1 dynamic-slice_bitcast_fusion.1
  351.3 8.8 %convolution_bitcast_fusion = f32[8,16,8,128]{3,2,1,0:T(8,128)S(1)} fusion(bf16[2048,4096]{0,1:T(8,128)(2,1)} %get-tuple-element.227, bf16[2048,64]{0,1:T(8,128)(2,1)S(1)} %get-tuple-element.325, bf16[2048,64]{0,1:T(8,128)(2,1)S(1)} %get-tuple-element.324), kind=kOutput, calls=%fused_computation.21 | convolution fusion | flops 1074790400 | bytes 17825792 | tf_op jit(solution)/shard_map/dot_general | solution.py:129
  360.1 0.8 copy.49
  361.0 11.1 %all-to-all-start.3 = ((f32[16,128,64]{1,2,0:T(8,128)}), f32[16,128,64]{1,2,0:T(8,128)S(1)}, u32[]{:S(2)}, u32[]{:S(2)}) async-start(f32[16,128,64]{1,2,0:T(8,128)} %bitcast.42), calls=%async_computation.3 | async-start | bytes 1048576 | tf_op jit(solution)/shard_map/all_to_all | solution.py:47
  372.1 0.0 copy-start.1
  372.1 21.0 %all-to-all-done.3 = f32[16,128,64]{1,2,0:T(8,128)S(1)} async-done(((f32[16,128,64]{1,2,0:T(8,128)}), f32[16,128,64]{1,2,0:T(8,128)S(1)}, u32[]{:S(2)}, u32[]{:S(2)}) %all-to-all-start.3) | async-done | bytes 524320 | tf_op jit(solution)/shard_map/all_to_all | solution.py:47
  393.2 0.7 fusion.20
  394.0 24.5 %all_to_all.26 = f32[16,128,64]{1,2,0:T(8,128)S(1)} all-to-all(f32[16,128,64]{1,2,0:T(8,128)S(1)} %broadcast_in_dim.62), channel_id=1, replica_groups=mesh['row'=32,'col_0'=8,'col_1'=2] {'col_0','col_1'}, dimensions={0} | all-to-all | bytes 1048576 | tf_op jit(solution)/shard_map/all_to_all | solution.py:25
  418.4 0.8 copy_bitcast_fusion
  419.2 0.0 copy-done.1
  (32 shorter events, 0.6 us)
Async XLA Ops:
  10.5 117.8 %copy-start.2 = (s32[32,32]{1,0:T(8,128)S(1)}, s32[32,32]{1,0:T(8,128)}, u32[]{:S(2)}) copy-start(s32[32,32]{1,0:T(8,128)} %param.10) | copy-start | bytes 12292
  10.5 34.2 %all-to-all-start = ((bf16[32,128,128]{1,2,0:T(8,128)(2,1)}), bf16[32,128,128]{1,2,0:T(8,128)(2,1)S(1)}, u32[]{:S(2)}, u32[]{:S(2)}) async-start(bf16[32,128,128]{1,2,0:T(8,128)(2,1)} %broadcast_in_dim.58), calls=%async_computation | async-start | bytes 2097152 | tf_op jit(solution)/shard_map/all_to_all | solution.py:25
  20.1 108.2 %all-reduce.3.cloned.1.call-start = ((), (), s32[]{:S(2)}) async-start(), calls=%async_computation.5 | async-start | bytes 1048576 | tf_op jit(solution)/shard_map/psum | solution.py:35
  46.5 142.4 %all-reduce.5.cloned.1.call-start = ((), (), s32[]{:S(2)}) async-start(), calls=%async_computation.6 | async-start | bytes 1048576 | tf_op jit(solution)/shard_map/psum | solution.py:35
  190.3 6.0 %copy-start.3 = (f32[2048]{0:T(1024)S(1)}, f32[2048]{0:T(1024)}, u32[]{:S(2)}) copy-start(f32[2048]{0:T(1024)} %param.11) | copy-start | bytes 24580
  219.5 18.2 %copy-start = (bf16[2048,128]{0,1:T(8,128)(2,1)S(1)}, bf16[2048,128]{0,1:T(8,128)(2,1)}, u32[]{:S(2)}) copy-start(bf16[2048,128]{0,1:T(8,128)(2,1)} %all-reduce.5.cloned.1.call-done) | copy-start | bytes 1572868
  229.3 28.8 %all-to-all-start.1 = ((f32[16,128,64]{1,2,0:T(8,128)}), f32[16,128,64]{1,2,0:T(8,128)S(1)}, u32[]{:S(2)}, u32[]{:S(2)}) async-start(f32[16,128,64]{1,2,0:T(8,128)} %bitcast.43), calls=%async_computation.1 | async-start | bytes 1048576 | tf_op jit(solution)/shard_map/all_to_all | solution.py:47
  237.6 112.7 %all-gather.2.cloned.1.call-start = ((), (), s32[]{:S(2)}) async-start(), calls=%async_computation.7 | async-start | bytes 8650752 | tf_op jit(solution)/shard_map/all_gather | solution.py:52
  361.0 32.2 %all-to-all-start.3 = ((f32[16,128,64]{1,2,0:T(8,128)}), f32[16,128,64]{1,2,0:T(8,128)S(1)}, u32[]{:S(2)}, u32[]{:S(2)}) async-start(f32[16,128,64]{1,2,0:T(8,128)} %bitcast.42), calls=%async_computation.3 | async-start | bytes 1048576 | tf_op jit(solution)/shard_map/all_to_all | solution.py:47
  372.1 47.2 %copy-start.1 = (f32[2048,64]{0,1:T(8,128)}, f32[2048,64]{0,1:T(8,128)S(1)}, u32[]{:S(2)}) copy-start(f32[2048,64]{0,1:T(8,128)S(1)} %copy_bitcast_fusion.1) | copy-start | bytes 1572868
Sparse Core Ops, SparseCore 0:
  46.7 81.5 all-reduce.2
  131.2 57.7 all-reduce.4
  284.5 65.7 all-gather.1
where the time goes:
time: 427 us; the launch traced here: 426 us
  waiting for transfers between devices  273 us (64%)
  blocking collectives  48.8 us (11%)
  matrix products  41.3 us (10%)
  starting transfers between devices  29 us (7%)
  local copies, waits for them, and re-layouts  14.4 us (3%)
  between operations  14 us (3%)
  other arithmetic  4.94 us (1%)
    psum x2, waiting for transfers between devices, broadcast_by_axis(): array = lax.psum(array, axis)  141 us
    all_gather x1, waiting for transfers between devices, broadcast(): lax.all_gather(array, axis)  65.9 us
    all_to_all x2, blocking collectives, copy_for_each(): return lax.all_to_all(copies, axis, split_axis=0, concat_axis=0, tiled=True)  48.8 us
    all_to_all x2, waiting for transfers between devices, sent_and_summed(): parts = lax.all_to_all(split_up(array, dim, count), axis, 0, 0, tiled=True)  41.3 us
    all_to_all x1, waiting for transfers between devices, copy_for_each(): return lax.all_to_all(copies, axis, split_axis=0, concat_axis=0, tiled=True)  24.6 us
    dot_general x8, matrix products, build(): lax.dot_general(row_slopes, cols, (((1,), (1,)), ((), ())), preferred_ele...  22.7 us
    all_to_all x2, starting transfers between devices, sent_and_summed(): parts = lax.all_to_all(split_up(array, dim, count), axis, 0, 0, tiled=True)  19.3 us
    all_to_all x1, starting transfers between devices, copy_for_each(): return lax.all_to_all(copies, axis, split_axis=0, concat_axis=0, tiled=True)  9.54 us
  transfers between devices with their start and end apart: 6, of which 6 were waited for; matrix products, arithmetic and copies ran while one was open for 0% of the time, Pallas kernels for 0%

commit v1 on v0

v1 whole, which is shorter than its diff:
```python
import jax
import jax.numpy as jnp
from jax import lax
from jax.experimental import pallas as pl
from jax.experimental.pallas import tpu as pltpu
from jax.sharding import PartitionSpec as P

NZ, NH, NL, NX, NU = 8, 2, 4, 4, 2
NY = NH * NL
ROWS = 128
HALF = ROWS // 2
SUBAP = 2048
SHARDS = NY * NX * NU
PIECES = NZ
TILE = NU * ROWS
TILES = SHARDS // NU
TILES_SENSOR = SUBAP // TILE
SLOTS = 16
CHUNK = 4
MESH = pl.DeviceIdType.MESH
damping = 0.4
f32, bf16 = jnp.float32, jnp.bfloat16


def low_lanes(shape):
    return lax.broadcasted_iota(jnp.int32, shape, 1) < HALF


def swap(v):
    return pltpu.roll(v, HALF, 1)


def kernel(
    joined, invb, target, noise, out1, out2,
    colb, rowp, srow, scol, xcol, cov, dist, acc, bsend, brecv, dsend, drecv,
    tgt, noi, low1, low2, cbuf, ebuf1, ebuf2,
    send_a, recv_a, send_r, recv_r, send_t, recv_t, send_n, recv_n, send_b, recv_b,
    send_c, recv_c, send_d, recv_d, send_e, recv_e, send_f, recv_f,
):
    row, col = lax.axis_index("row"), lax.axis_index("col")
    z, h = col // NH, col % NH
    l, x, u = row // (NX * NU), row // NU % NX, row % NU
    y = h * NL + l

    def rowid(yy, xx, uu):
        return yy % NL * (NX * NU) + xx * NU + uu

    def colid(zz, yy):
        return zz * NH + yy // NL

    def at(zz, yy, xx, uu):
        return rowid(yy, xx, uu), colid(zz, yy)

    def shard(yy, xx, uu):
        return (yy * NX + xx) * NU + uu

    def remote(src, dst, ssem, rsem, dev):
        return pltpu.make_async_remote_copy(
            src_ref=src, dst_ref=dst, send_sem=ssem, recv_sem=rsem, device_id=dev, device_id_type=MESH
        )

    def put_maybe_self(src, dst, ssem, rsem, dev):
        mine = (dev[0] == row) & (dev[1] == col)

        @pl.when(mine)
        def _():
            pltpu.make_async_copy(src, dst, rsem).start()

        @pl.when(jnp.logical_not(mine))
        def _():
            remote(src, dst, ssem, rsem, dev).start()

    me = shard(y, x, u)
    here = (row, col)
    xl, xr, xo = (x + NX - 1) % NX, (x + 1) % NX, (x + 2) % NX
    order = [0] + [d for k in range(1, NY // 2) for d in (k, -k)] + [NY // 2]
    ys = [(y + d + NY) % NY for d in order]
    zs = [(z + d) % NZ for d in range(1, NZ)]

    barrier = pltpu.get_barrier_semaphore()
    near = [at(zz, y, x, u) for zz in zs] + [at(z, yy, x, u) for yy in ys[1:]]
    near += [at(z, y, xl, u), at(z, y, xr, u), at(z, y, x, 1 - u)]
    for dev in near:
        pl.semaphore_signal(barrier, inc=1, device_id=dev, device_id_type=MESH)
    pl.semaphore_wait(barrier, len(near))

    def plane_gather(src, buf, ssem, rsem):
        count = [0]
        sent = []

        def send(s_src, s, dev, cond=None):
            k = count[0]
            count[0] += 1
            copy = remote(s_src, buf.at[s], ssem.at[k], rsem.at[s], dev)
            sent.append((copy, cond))
            if cond is None:
                copy.start()
            else:
                pl.when(cond)(copy.start)

        def wait(s):
            remote(src, buf.at[s], ssem.at[0], rsem.at[s], here).wait_recv()

        for yy in ys[1:]:
            send(src, me, at(z, yy, x, u))
        for i, yy in enumerate(ys):
            s = shard(yy, x, u)
            if i:
                wait(s)
            s_src = buf.at[s] if i else src
            for dev in (at(z, y, xl, u), at(z, y, xr, u), at(z, y, x, 1 - u)):
                send(s_src, s, dev)
        for yy in ys:
            even = yy % 2 == 0
            sl, sr = shard(yy, xl, u), shard(yy, xr, u)
            wait(sl)
            send(buf.at[sl], sl, at(z, y, xr, u), even)
            send(buf.at[sl], sl, at(z, y, x, 1 - u))
            wait(sr)
            send(buf.at[sr], sr, at(z, y, xl, u), jnp.logical_not(even))
            send(buf.at[sr], sr, at(z, y, x, 1 - u))
        for yy in ys:
            s = shard(yy, xo, u)
            wait(s)
            send(buf.at[s], s, at(z, y, x, 1 - u))
        for yy in ys:
            for xx in range(NX):
                wait(shard(yy, xx, 1 - u))

        def drain():
            for copy, cond in sent:
                if cond is None:
                    copy.wait_send()
                else:
                    pl.when(cond)(copy.wait_send)

        return drain

    mine_s = joined.at[pl.ds(0, HALF)]
    for k, zz in enumerate(zs):
        remote(mine_s, rowp.at[z], send_r.at[k], recv_r.at[z], at(zz, y, x, u)).start()
    drain_a = plane_gather(joined, colb, send_a, recv_a)

    source = (l == z // 2) & (x // 2 == z % 2)
    owner_dev = []
    for xx in range(NX):
        for uu in range(NU):
            slot = h * (NX * NU) + xx * NU + uu
            dev = ((2 * u + h) * (NX * NU) + xx * NU + uu, z * NH + x % NH)
            owner_dev.append((slot, dev))

    @pl.when(source)
    def _():
        for k, (slot, dev) in enumerate(owner_dev):
            off = pl.multiple_of(slot * ROWS, ROWS)
            put_maybe_self(target.at[pl.ds(off, ROWS)], tgt, send_t.at[k], recv_t, dev)
            put_maybe_self(noise.at[slot], noi, send_n.at[k], recv_n, dev)

    colb[me] = joined[...]

    def unpack(s, carry):
        base = pl.multiple_of(s * ROWS, ROWS)
        sp = colb[s, :HALF, :]
        xp = colb[s, HALF:, :]
        scol[pl.ds(base, HALF), :] = sp
        scol[pl.ds(pl.multiple_of(base + HALF, HALF), HALF), :] = swap(sp.astype(f32)).astype(bf16)
        xcol[pl.ds(base, HALF), :] = xp
        xcol[pl.ds(pl.multiple_of(base + HALF, HALF), HALF), :] = swap(xp.astype(f32)).astype(bf16)
        return carry

    lax.fori_loop(0, SHARDS, unpack, 0)
    for zz in zs:
        remote(mine_s, rowp.at[zz], send_r.at[0], recv_r.at[zz], here).wait_recv()
    rowp[z] = joined[:HALF, :]
    keep = low_lanes((HALF, ROWS))
    for j in range(PIECES):
        v = rowp[j].astype(f32) * (1.0 / 16384.0)
        srow[pl.ds(j * ROWS, HALF), :] = jnp.where(keep, v, 0.0).astype(bf16)
        srow[pl.ds(j * ROWS + HALF, HALF), :] = jnp.where(keep, swap(v), 0.0).astype(bf16)

    p0 = (l % 2 * (NX * NU) + x * NU + u) * ROWS
    base_d = (
        p0 + lax.broadcasted_iota(jnp.int32, (ROWS, TILE), 0) - lax.broadcasted_iota(jnp.int32, (ROWS, TILE), 1)
    )
    for t in range(TILES_SENSOR):
        dist[t] = jnp.abs(base_d - t * TILE).astype(f32)

    contract_last = (((1,), (1,)), ((), ()))

    def pack_piece(j):
        r = pl.multiple_of(j * ROWS, ROWS)
        lo = acc[pl.ds(r, HALF), :]
        hi = acc[pl.ds(pl.multiple_of(r + HALF, HALF), HALF), :]
        return jnp.where(keep, lo, swap(hi))

    def send_piece(j, sbuf, rbuf, ssem, rsem):
        sbuf[j] = pack_piece(j)

        @pl.when(j != z)
        def _():
            remote(sbuf.at[j], rbuf.at[z], ssem.at[j], rsem.at[z], at(j, y, x, u)).start()

    for c in range(PIECES // CHUNK):
        span = pl.ds(c * CHUNK * ROWS, CHUNK * ROWS)
        acc[span, :] = jnp.zeros((CHUNK * ROWS, ROWS), f32)

        def build(t, carry):
            cols = pl.ds(pl.multiple_of(t * TILE, TILE), TILE)
            raw = lax.dot_general(srow[span, :], scol[cols, :], contract_last, preferred_element_type=f32)
            d = dist[t % TILES_SENSOR]
            parts = []
            for i in range(CHUNK):
                j = c * CHUNK + i
                inv = invb[NL * j + y // 2, NL * z + t // TILES_SENSOR]
                taper = jnp.maximum(0.0, 1.0 - d * inv)
                parts.append((taper * raw[i * ROWS : (i + 1) * ROWS, :]).astype(bf16))
            entry = jnp.concatenate(parts, axis=0)
            cov[t, span, :] = entry
            acc[span, :] += jnp.dot(entry, xcol[cols, :], preferred_element_type=f32)
            return carry

        lax.fori_loop(0, TILES, build, 0)
        for i in range(CHUNK):
            send_piece(c * CHUNK + i, bsend, brecv, send_b, recv_b)

    def collected(sbuf, rbuf, rsem):
        total = sbuf[z]
        for zz in zs:
            remote(sbuf.at[0], rbuf.at[zz], send_b.at[0], rsem.at[zz], here).wait_recv()
            total = total + rbuf[zz]
        return total

    remote(target.at[pl.ds(0, ROWS)], tgt, send_t.at[0], recv_t, here).wait_recv()
    remote(noise.at[0], noi, send_n.at[0], recv_n, here).wait_recv()
    s_own = joined[:HALF, :].astype(f32)
    x_own = joined[HALF:, :].astype(f32)
    sq = s_own * s_own
    raw_lo = jnp.sum(jnp.where(keep, sq, 0.0), axis=1, keepdims=True)
    raw_hi = jnp.sum(jnp.where(keep, 0.0, sq), axis=1, keepdims=True)
    raw_own = jnp.where(keep, raw_lo, raw_hi) * (1.0 / 16384.0)
    noise_t = jnp.transpose(jnp.broadcast_to(noi[0:1, :], (ROWS, ROWS)))
    noise_own = jnp.where(keep, noise_t[:HALF], noise_t[HALF:])
    tgt_f = tgt[...].astype(f32)
    tgt_own = jnp.concatenate([tgt_f[:HALF], tgt_f[HALF:]], axis=1)
    diag = raw_own + noise_own
    weight = damping / diag
    extra = diag.astype(bf16).astype(f32) - raw_own.astype(bf16).astype(f32)

    first = x_own + weight * (tgt_own - (collected(bsend, brecv, recv_b) + extra * x_own))
    low1[...] = first.astype(bf16)

    out_row = (z // 2) * (NX * NU) + (z % 2 * 2 + h) * NU + l // 2
    slot_me = l % 2 * (NX * NU) + x * NU + u
    outs = [(zz * NH + hh) for zz in range(NZ) for hh in range(NH)]

    def spread(src, buf, ssem, rsem):
        for k, cc in enumerate(outs):
            put_maybe_self(src, buf.at[slot_me], ssem.at[k], rsem.at[slot_me], (out_row, cc))

    def spread_sent(src, buf, ssem, rsem):
        for k, cc in enumerate(outs):
            @pl.when(jnp.logical_not((out_row == row) & (cc == col)))
            def _():
                remote(src, buf.at[slot_me], ssem.at[k], rsem.at[slot_me], (out_row, cc)).wait_send()

    def unpack_out(src, buf, rsem, out):
        for s in range(SLOTS):
            remote(src, buf.at[s], send_e.at[0], rsem.at[s], here).wait_recv()
            v = buf[s].astype(f32)
            out[pl.ds(s * ROWS, HALF), :] = v[:, :HALF].astype(bf16)
            out[pl.ds(s * ROWS + HALF, HALF), :] = swap(v)[:, :HALF].astype(bf16)

    drain_c = plane_gather(low1, cbuf, send_c, recv_c)
    spread(low1, ebuf1, send_e, recv_e)
    cbuf[me] = low1[...]

    def unpack_first(s, carry):
        base = pl.multiple_of(s * ROWS, ROWS)
        xp = cbuf[s]
        xcol[pl.ds(base, HALF), :] = xp
        xcol[pl.ds(pl.multiple_of(base + HALF, HALF), HALF), :] = swap(xp.astype(f32)).astype(bf16)
        return carry

    lax.fori_loop(0, SHARDS, unpack_first, 0)

    for c in range(PIECES // CHUNK):
        span = pl.ds(c * CHUNK * ROWS, CHUNK * ROWS)
        acc[span, :] = jnp.zeros((CHUNK * ROWS, ROWS), f32)

        def multiply(t, carry):
            cols = pl.ds(pl.multiple_of(t * TILE, TILE), TILE)
            acc[span, :] += jnp.dot(cov[t, span, :], xcol[cols, :], preferred_element_type=f32)
            return carry

        lax.fori_loop(0, TILES, multiply, 0)
        for i in range(CHUNK):
            send_piece(c * CHUNK + i, dsend, drecv, send_d, recv_d)

    product1 = collected(dsend, drecv, recv_d) + extra * first.astype(bf16).astype(f32)
    low2[...] = (first + weight * (tgt_own - product1)).astype(bf16)
    spread(low2, ebuf2, send_f, recv_f)
    unpack_out(low1, ebuf1, recv_e, out1)
    unpack_out(low2, ebuf2, recv_f, out2)

    drain_a()
    drain_c()
    for k, zz in enumerate(zs):
        remote(mine_s, rowp.at[z], send_r.at[k], recv_r.at[z], at(zz, y, x, u)).wait_send()

    @pl.when(source)
    def _():
        for k, (slot, dev) in enumerate(owner_dev):
            off = pl.multiple_of(slot * ROWS, ROWS)

            @pl.when(jnp.logical_not((dev[0] == row) & (dev[1] == col)))
            def _():
                remote(target.at[pl.ds(off, ROWS)], tgt, send_t.at[k], recv_t, dev).wait_send()
                remote(noise.at[slot], noi, send_n.at[k], recv_n, dev).wait_send()

    for j in range(PIECES):
        @pl.when(j != z)
        def _():
            remote(bsend.at[j], brecv.at[z], send_b.at[j], recv_b.at[z], at(j, y, x, u)).wait_send()
            remote(dsend.at[j], drecv.at[z], send_d.at[j], recv_d.at[z], at(j, y, x, u)).wait_send()

    spread_sent(low1, ebuf1, send_e, recv_e)
    spread_sent(low2, ebuf2, send_f, recv_f)


def pack(a):
    return jnp.concatenate([a[:HALF], a[HALF:]], axis=1)


def on_device(telemetry, scales, bands, noise, start, target):
    slopes = (telemetry.astype(f32) * scales.astype(f32)[:, None] / 128.0).astype(bf16)
    joined = jnp.concatenate([pack(slopes), pack(start)], axis=0)
    index = jnp.arange(bands.shape[0], dtype=jnp.int32)
    sym = jnp.where(index[:, None] <= index[None, :], bands, bands.T).astype(f32)
    invb = 1.0 / sym
    noise = jnp.broadcast_to(noise.reshape(SLOTS, 1, ROWS), (SLOTS, 8, ROWS))
    vmem = pl.BlockSpec(memory_space=pltpu.VMEM)
    dma, gathers = pltpu.SemaphoreType.DMA, SHARDS + 8
    out = jax.ShapeDtypeStruct(target.shape, bf16)
    packed = (HALF, ROWS)
    first, second = pl.pallas_call(
        kernel,
        out_shape=(out, out),
        in_specs=[vmem, pl.BlockSpec(memory_space=pltpu.SMEM), vmem, vmem],
        out_specs=(vmem, vmem),
        scratch_shapes=[
            pltpu.VMEM((SHARDS, ROWS, ROWS), bf16),
            pltpu.VMEM((PIECES, *packed), bf16),
            pltpu.VMEM((PIECES * ROWS, ROWS), bf16),
            pltpu.VMEM((SHARDS * ROWS, ROWS), bf16),
            pltpu.VMEM((SHARDS * ROWS, ROWS), bf16),
            pltpu.VMEM((TILES, PIECES * ROWS, TILE), bf16),
            pltpu.VMEM((TILES_SENSOR, ROWS, TILE), f32),
            pltpu.VMEM((PIECES * ROWS, ROWS), f32),
            pltpu.VMEM((PIECES, *packed), f32),
            pltpu.VMEM((PIECES, *packed), f32),
            pltpu.VMEM((PIECES, *packed), f32),
            pltpu.VMEM((PIECES, *packed), f32),
            pltpu.VMEM((ROWS, HALF), bf16),
            pltpu.VMEM((8, ROWS), f32),
            pltpu.VMEM(packed, bf16),
            pltpu.VMEM(packed, bf16),
            pltpu.VMEM((SHARDS, *packed), bf16),
            pltpu.VMEM((SLOTS, *packed), bf16),
            pltpu.VMEM((SLOTS, *packed), bf16),
            dma((gathers + 8,)), dma((SHARDS,)),
            dma((NZ,)), dma((NZ,)),
            dma((8,)), dma,
            dma((8,)), dma,
            dma((NZ,)), dma((NZ,)),
            dma((gathers + 8,)), dma((SHARDS,)),
            dma((NZ,)), dma((NZ,)),
            dma((SLOTS,)), dma((SLOTS,)),
            dma((SLOTS,)), dma((SLOTS,)),
        ],
        compiler_params=pltpu.CompilerParams(
            collective_id=0, has_side_effects=True, vmem_limit_bytes=60 * 2**20
        ),
    )(joined, invb, target, noise)
    return first.astype(f32), second.astype(f32)


def solution(mesh):
    placed = (P(("col", "row"), None), P(("col", "row")), P(), P("row"), P(("col", "row"), None), P("row", None))
    return jax.shard_map(
        on_device,
        mesh=mesh,
        in_specs=placed,
        out_specs=(P("row", None), P("row", None)),
        check_vma=False,
    )
```

time: 427 us -> 144 us (0.34)
  the two profiles are of different devices: /device:TPU:10 before, /device:TPU:89 now
where the time goes in v1:
time: 144 us; the launch traced here: 143 us
  Pallas kernels  134 us (93%)
  local copies, waits for them, and re-layouts  7.25 us (5%)
    pallas_call x1, Pallas kernels, on_device(): pl.pallas_call(kernel, out_shape=(out, out), in_specs=[vmem, pl.BlockSpec...  134 us
    unnamed x20, local copies, waits for them, and re-layouts  6.44 us

profile of v1, /device:TPU:89, one launch (start us, length us, event | category | flops | bytes accessed | tf_op | source)
XLA Modules:
  0.0 143.3 jit_solution(6016137368164491415)
XLA Ops:
  0.6 0.0 copy-start.6
  0.6 0.6 copy-done.6
  1.3 0.0 copy-start.2
  1.3 0.9 copy.18
  2.2 0.0 copy-done.2
  2.2 0.0 copy-start.4
  2.2 0.6 fusion.1.invb
  2.8 0.1 copy-done.4
  2.9 0.0 copy-start.3
  2.9 0.1 copy.15
  3.0 0.0 copy-start.1
  3.0 0.1 multiply_convert_fusion
  3.1 0.5 copy-done.3
  3.6 0.1 fusion.3
  3.7 0.1 copy.22
  3.8 0.1 copy.23
  3.9 0.0 copy-start.5
  3.9 0.7 maximum_maximum_fusion.joined
  4.6 0.0 copy-done.5
  4.6 0.6 broadcast_in_dim.5.noise
  5.3 0.0 copy-done.1
  5.3 1.0 copy.19.target
  6.3 133.9 %shard_map.77 = (bf16[2048,64]{1,0:T(8,128)(2,1)}, bf16[2048,64]{1,0:T(8,128)(2,1)}) custom-call(bf16[128,128]{1,0:T(8,128)(2,1)} %maximum_maximum_fusion.joined, f32[32,32]{1,0:T(8,128)} %fusion.1.invb, bf16[2048,64]{1,0:T(8,128)(2,1)} %copy.19.target, f32[16,8,128]{2,1,0:T(8,128)} %broadcast_in_dim.5.noise), custom_call_target="tpu_custom_call" | custom-call | tf_op jit(solution)/shard_map/pallas_call | solution.py:345
  140.2 0.0 copy-start
  140.2 2.1 %copy.20 = f32[2048,64]{0,1:T(8,128)} copy(bf16[2048,64]{1,0:T(8,128)(2,1)} %get-tuple-element.4) | data formatting | bytes 786432
  142.3 0.0 copy-done
  142.3 1.0 copy.21
  (3 shorter events, 0.0 us)
Async XLA Ops:
  0.6 0.7 copy-start.6
  1.3 0.9 copy-start.2
  2.2 0.8 copy-start.4
  2.9 0.7 copy-start.3
  3.0 2.2 %copy-start.1 = (bf16[2048,64]{0,1:T(8,128)(2,1)S(1)}, bf16[2048,64]{0,1:T(8,128)(2,1)}, u32[]{:S(2)}) copy-start(bf16[2048,64]{0,1:T(8,128)(2,1)} %param.11) | copy-start | bytes 786436
  3.9 0.7 copy-start.5
  140.2 2.1 %copy-start = (bf16[2048,64]{1,0:T(8,128)(2,1)S(1)}, bf16[2048,64]{1,0:T(8,128)(2,1)}, u32[]{:S(2)}) copy-start(bf16[2048,64]{1,0:T(8,128)(2,1)} %get-tuple-element.5) | copy-start | bytes 786436

commit v2 on v1

--- a/solution.py
+++ b/solution.py
@@ -22,18 +22,10 @@
 f32, bf16 = jnp.float32, jnp.bfloat16
 
 
-def low_lanes(shape):
-    return lax.broadcasted_iota(jnp.int32, shape, 1) < HALF
-
-
-def swap(v):
-    return pltpu.roll(v, HALF, 1)
-
-
 def kernel(
-    joined, invb, target, noise, out1, out2,
-    colb, rowp, srow, scol, xcol, cov, dist, acc, bsend, brecv, dsend, drecv,
-    tgt, noi, low1, low2, cbuf, ebuf1, ebuf2,
+    telemetry, scales, bands, noise, start, target, out1, out2,
+    joined, colb, rowp, srow, inv, cov, dist, acc, bsend, brecv, dsend, drecv,
+    tgt, noises, noi, low1, low2, cbuf, ebuf1, ebuf2,
     send_a, recv_a, send_r, recv_r, send_t, recv_t, send_n, recv_n, send_b, recv_b,
     send_c, recv_c, send_d, recv_d, send_e, recv_e, send_f, recv_f,
 ):
@@ -82,6 +74,12 @@
     near += [at(z, y, xl, u), at(z, y, xr, u), at(z, y, x, 1 - u)]
     for dev in near:
         pl.semaphore_signal(barrier, inc=1, device_id=dev, device_id_type=MESH)
+
+    slopes = telemetry[...].astype(f32) * scales[...].astype(f32) * (1.0 / 128.0)
+    joined[:HALF, :] = slopes.astype(bf16)
+    joined[HALF:, :] = start[...]
+    for s in range(SLOTS):
+        noises[s] = jnp.broadcast_to(noise[s : s + 1, :], (8, ROWS))
     pl.semaphore_wait(barrier, len(near))
 
     def plane_gather(src, buf, ssem, rsem):
@@ -141,6 +139,9 @@
         remote(mine_s, rowp.at[z], send_r.at[k], recv_r.at[z], at(zz, y, x, u)).start()
     drain_a = plane_gather(joined, colb, send_a, recv_a)
 
+    def target_part(slot):
+        return target.at[:, pl.ds(pl.multiple_of(slot * ROWS, ROWS), ROWS)]
+
     source = (l == z // 2) & (x // 2 == z % 2)
     owner_dev = []
     for xx in range(NX):
@@ -152,31 +153,14 @@
     @pl.when(source)
     def _():
         for k, (slot, dev) in enumerate(owner_dev):
-            off = pl.multiple_of(slot * ROWS, ROWS)
-            put_maybe_self(target.at[pl.ds(off, ROWS)], tgt, send_t.at[k], recv_t, dev)
-            put_maybe_self(noise.at[slot], noi, send_n.at[k], recv_n, dev)
-
-    colb[me] = joined[...]
-
-    def unpack(s, carry):
-        base = pl.multiple_of(s * ROWS, ROWS)
-        sp = colb[s, :HALF, :]
-        xp = colb[s, HALF:, :]
-        scol[pl.ds(base, HALF), :] = sp
-        scol[pl.ds(pl.multiple_of(base + HALF, HALF), HALF), :] = swap(sp.astype(f32)).astype(bf16)
-        xcol[pl.ds(base, HALF), :] = xp
-        xcol[pl.ds(pl.multiple_of(base + HALF, HALF), HALF), :] = swap(xp.astype(f32)).astype(bf16)
-        return carry
-
-    lax.fori_loop(0, SHARDS, unpack, 0)
-    for zz in zs:
-        remote(mine_s, rowp.at[zz], send_r.at[0], recv_r.at[zz], here).wait_recv()
-    rowp[z] = joined[:HALF, :]
-    keep = low_lanes((HALF, ROWS))
+            put_maybe_self(target_part(slot), tgt, send_t.at[k], recv_t, dev)
+            put_maybe_self(noises.at[slot], noi, send_n.at[k], recv_n, dev)
+
     for j in range(PIECES):
-        v = rowp[j].astype(f32) * (1.0 / 16384.0)
-        srow[pl.ds(j * ROWS, HALF), :] = jnp.where(keep, v, 0.0).astype(bf16)
-        srow[pl.ds(j * ROWS + HALF, HALF), :] = jnp.where(keep, swap(v), 0.0).astype(bf16)
+        for k in range(NL):
+            a, b = NL * j + y // 2, NL * z + k
+            band = bands[jnp.minimum(a, b), jnp.maximum(a, b)].astype(f32)
+            inv[j * NL + k] = 1.0 / jnp.full((1, TILE), band, f32)
 
     p0 = (l % 2 * (NX * NU) + x * NU + u) * ROWS
     base_d = (
@@ -185,13 +169,23 @@
     for t in range(TILES_SENSOR):
         dist[t] = jnp.abs(base_d - t * TILE).astype(f32)
 
+    colb[me] = joined[...]
+    for zz in zs:
+        remote(mine_s, rowp.at[zz], send_r.at[0], recv_r.at[zz], here).wait_recv()
+    rowp[z] = joined[:HALF, :]
+    for j in range(PIECES):
+        v = rowp[j].astype(f32) * (1.0 / 16384.0)
+        srow[pl.ds(j * ROWS, ROWS), :] = jnp.transpose(v).astype(bf16)
+
     contract_last = (((1,), (1,)), ((), ()))
 
     def pack_piece(j):
-        r = pl.multiple_of(j * ROWS, ROWS)
-        lo = acc[pl.ds(r, HALF), :]
-        hi = acc[pl.ds(pl.multiple_of(r + HALF, HALF), HALF), :]
-        return jnp.where(keep, lo, swap(hi))
+        return jnp.transpose(acc[pl.ds(pl.multiple_of(j * ROWS, ROWS), ROWS), :])
+
+    def pair(ref, t, part):
+        return jnp.concatenate([ref[NU * t + i, part, :] for i in range(NU)], axis=1)
+
+    slope_rows, panel_rows = slice(0, HALF), slice(HALF, ROWS)
 
     def send_piece(j, sbuf, rbuf, ssem, rsem):
         sbuf[j] = pack_piece(j)
@@ -202,21 +196,21 @@
 
     for c in range(PIECES // CHUNK):
         span = pl.ds(c * CHUNK * ROWS, CHUNK * ROWS)
-        acc[span, :] = jnp.zeros((CHUNK * ROWS, ROWS), f32)
+        acc[span, :] = jnp.zeros((CHUNK * ROWS, HALF), f32)
 
         def build(t, carry):
-            cols = pl.ds(pl.multiple_of(t * TILE, TILE), TILE)
-            raw = lax.dot_general(srow[span, :], scol[cols, :], contract_last, preferred_element_type=f32)
+            raw = jnp.dot(srow[span, :], pair(colb, t, slope_rows), preferred_element_type=f32)
             d = dist[t % TILES_SENSOR]
             parts = []
             for i in range(CHUNK):
                 j = c * CHUNK + i
-                inv = invb[NL * j + y // 2, NL * z + t // TILES_SENSOR]
-                taper = jnp.maximum(0.0, 1.0 - d * inv)
+                taper = jnp.maximum(0.0, 1.0 - d * inv[j * NL + t // TILES_SENSOR])
                 parts.append((taper * raw[i * ROWS : (i + 1) * ROWS, :]).astype(bf16))
             entry = jnp.concatenate(parts, axis=0)
             cov[t, span, :] = entry
-            acc[span, :] += jnp.dot(entry, xcol[cols, :], preferred_element_type=f32)
+            acc[span, :] += lax.dot_general(
+                entry, pair(colb, t, panel_rows), contract_last, preferred_element_type=f32
+            )
             return carry
 
         lax.fori_loop(0, TILES, build, 0)
@@ -230,21 +224,15 @@
             total = total + rbuf[zz]
         return total
 
-    remote(target.at[pl.ds(0, ROWS)], tgt, send_t.at[0], recv_t, here).wait_recv()
-    remote(noise.at[0], noi, send_n.at[0], recv_n, here).wait_recv()
+    remote(target_part(0), tgt, send_t.at[0], recv_t, here).wait_recv()
+    remote(noises.at[0], noi, send_n.at[0], recv_n, here).wait_recv()
     s_own = joined[:HALF, :].astype(f32)
     x_own = joined[HALF:, :].astype(f32)
-    sq = s_own * s_own
-    raw_lo = jnp.sum(jnp.where(keep, sq, 0.0), axis=1, keepdims=True)
-    raw_hi = jnp.sum(jnp.where(keep, 0.0, sq), axis=1, keepdims=True)
-    raw_own = jnp.where(keep, raw_lo, raw_hi) * (1.0 / 16384.0)
-    noise_t = jnp.transpose(jnp.broadcast_to(noi[0:1, :], (ROWS, ROWS)))
-    noise_own = jnp.where(keep, noise_t[:HALF], noise_t[HALF:])
-    tgt_f = tgt[...].astype(f32)
-    tgt_own = jnp.concatenate([tgt_f[:HALF], tgt_f[HALF:]], axis=1)
-    diag = raw_own + noise_own
+    raw_own = jnp.sum(s_own * s_own, axis=0, keepdims=True) * (1.0 / 16384.0)
+    diag = raw_own + noi[0:1, :]
     weight = damping / diag
     extra = diag.astype(bf16).astype(f32) - raw_own.astype(bf16).astype(f32)
+    tgt_own = tgt[...].astype(f32)
 
     first = x_own + weight * (tgt_own - (collected(bsend, brecv, recv_b) + extra * x_own))
     low1[...] = first.astype(bf16)
@@ -266,30 +254,20 @@
     def unpack_out(src, buf, rsem, out):
         for s in range(SLOTS):
             remote(src, buf.at[s], send_e.at[0], rsem.at[s], here).wait_recv()
-            v = buf[s].astype(f32)
-            out[pl.ds(s * ROWS, HALF), :] = v[:, :HALF].astype(bf16)
-            out[pl.ds(s * ROWS + HALF, HALF), :] = swap(v)[:, :HALF].astype(bf16)
+            out[:, pl.ds(s * ROWS, ROWS)] = buf[s]
 
     drain_c = plane_gather(low1, cbuf, send_c, recv_c)
     spread(low1, ebuf1, send_e, recv_e)
     cbuf[me] = low1[...]
 
-    def unpack_first(s, carry):
-        base = pl.multiple_of(s * ROWS, ROWS)
-        xp = cbuf[s]
-        xcol[pl.ds(base, HALF), :] = xp
-        xcol[pl.ds(pl.multiple_of(base + HALF, HALF), HALF), :] = swap(xp.astype(f32)).astype(bf16)
-        return carry
-
-    lax.fori_loop(0, SHARDS, unpack_first, 0)
-
     for c in range(PIECES // CHUNK):
         span = pl.ds(c * CHUNK * ROWS, CHUNK * ROWS)
-        acc[span, :] = jnp.zeros((CHUNK * ROWS, ROWS), f32)
+        acc[span, :] = jnp.zeros((CHUNK * ROWS, HALF), f32)
 
         def multiply(t, carry):
-            cols = pl.ds(pl.multiple_of(t * TILE, TILE), TILE)
-            acc[span, :] += jnp.dot(cov[t, span, :], xcol[cols, :], preferred_element_type=f32)
+            acc[span, :] += lax.dot_general(
+                cov[t, span, :], pair(cbuf, t, slice(None)), contract_last, preferred_element_type=f32
+            )
             return carry
 
         lax.fori_loop(0, TILES, multiply, 0)
@@ -310,12 +288,10 @@
     @pl.when(source)
     def _():
         for k, (slot, dev) in enumerate(owner_dev):
-            off = pl.multiple_of(slot * ROWS, ROWS)
-
             @pl.when(jnp.logical_not((dev[0] == row) & (dev[1] == col)))
             def _():
-                remote(target.at[pl.ds(off, ROWS)], tgt, send_t.at[k], recv_t, dev).wait_send()
-                remote(noise.at[slot], noi, send_n.at[k], recv_n, dev).wait_send()
+                remote(target_part(slot), tgt, send_t.at[k], recv_t, dev).wait_send()
+                remote(noises.at[slot], noi, send_n.at[k], recv_n, dev).wait_send()
 
     for j in range(PIECES):
         @pl.when(j != z)
@@ -327,52 +303,43 @@
     spread_sent(low2, ebuf2, send_f, recv_f)
 
 
-def pack(a):
-    return jnp.concatenate([a[:HALF], a[HALF:]], axis=1)
-
-
 def on_device(telemetry, scales, bands, noise, start, target):
-    slopes = (telemetry.astype(f32) * scales.astype(f32)[:, None] / 128.0).astype(bf16)
-    joined = jnp.concatenate([pack(slopes), pack(start)], axis=0)
-    index = jnp.arange(bands.shape[0], dtype=jnp.int32)
-    sym = jnp.where(index[:, None] <= index[None, :], bands, bands.T).astype(f32)
-    invb = 1.0 / sym
-    noise = jnp.broadcast_to(noise.reshape(SLOTS, 1, ROWS), (SLOTS, 8, ROWS))
     vmem = pl.BlockSpec(memory_space=pltpu.VMEM)
-    dma, gathers = pltpu.SemaphoreType.DMA, SHARDS + 8
-    out = jax.ShapeDtypeStruct(target.shape, bf16)
-    packed = (HALF, ROWS)
+    dma, gathers = pltpu.SemaphoreType.DMA, SHARDS + 16
+    out = jax.ShapeDtypeStruct(target.shape[::-1], bf16)
+    part = (HALF, ROWS)
     first, second = pl.pallas_call(
         kernel,
         out_shape=(out, out),
-        in_specs=[vmem, pl.BlockSpec(memory_space=pltpu.SMEM), vmem, vmem],
+        in_specs=[vmem, vmem, pl.BlockSpec(memory_space=pltpu.SMEM), vmem, vmem, vmem],
         out_specs=(vmem, vmem),
         scratch_shapes=[
+            pltpu.VMEM((ROWS, ROWS), bf16),
             pltpu.VMEM((SHARDS, ROWS, ROWS), bf16),
-            pltpu.VMEM((PIECES, *packed), bf16),
-            pltpu.VMEM((PIECES * ROWS, ROWS), bf16),
-            pltpu.VMEM((SHARDS * ROWS, ROWS), bf16),
-            pltpu.VMEM((SHARDS * ROWS, ROWS), bf16),
+            pltpu.VMEM((PIECES, *part), bf16),
+            pltpu.VMEM((PIECES * ROWS, HALF), bf16),
+            pltpu.VMEM((PIECES * NL, 1, TILE), f32),
             pltpu.VMEM((TILES, PIECES * ROWS, TILE), bf16),
             pltpu.VMEM((TILES_SENSOR, ROWS, TILE), f32),
-            pltpu.VMEM((PIECES * ROWS, ROWS), f32),
-            pltpu.VMEM((PIECES, *packed), f32),
-            pltpu.VMEM((PIECES, *packed), f32),
-            pltpu.VMEM((PIECES, *packed), f32),
-            pltpu.VMEM((PIECES, *packed), f32),
-            pltpu.VMEM((ROWS, HALF), bf16),
+            pltpu.VMEM((PIECES * ROWS, HALF), f32),
+            pltpu.VMEM((PIECES, *part), f32),
+            pltpu.VMEM((PIECES, *part), f32),
+            pltpu.VMEM((PIECES, *part), f32),
+            pltpu.VMEM((PIECES, *part), f32),
+            pltpu.VMEM(part, bf16),
+            pltpu.VMEM((SLOTS, 8, ROWS), f32),
             pltpu.VMEM((8, ROWS), f32),
-            pltpu.VMEM(packed, bf16),
-            pltpu.VMEM(packed, bf16),
-            pltpu.VMEM((SHARDS, *packed), bf16),
-            pltpu.VMEM((SLOTS, *packed), bf16),
-            pltpu.VMEM((SLOTS, *packed), bf16),
-            dma((gathers + 8,)), dma((SHARDS,)),
+            pltpu.VMEM(part, bf16),
+            pltpu.VMEM(part, bf16),
+            pltpu.VMEM((SHARDS, *part), bf16),
+            pltpu.VMEM((SLOTS, *part), bf16),
+            pltpu.VMEM((SLOTS, *part), bf16),
+            dma((gathers,)), dma((SHARDS,)),
             dma((NZ,)), dma((NZ,)),
             dma((8,)), dma,
             dma((8,)), dma,
             dma((NZ,)), dma((NZ,)),
-            dma((gathers + 8,)), dma((SHARDS,)),
+            dma((gathers,)), dma((SHARDS,)),
             dma((NZ,)), dma((NZ,)),
             dma((SLOTS,)), dma((SLOTS,)),
             dma((SLOTS,)), dma((SLOTS,)),
@@ -380,8 +347,8 @@
         compiler_params=pltpu.CompilerParams(
             collective_id=0, has_side_effects=True, vmem_limit_bytes=60 * 2**20
         ),
-    )(joined, invb, target, noise)
-    return first.astype(f32), second.astype(f32)
+    )(telemetry.T, scales.reshape(1, ROWS), bands, noise.reshape(SLOTS, ROWS), start.T, target.T)
+    return first.T.astype(f32), second.T.astype(f32)
 
 
 def solution(mesh):

time: 144 us -> 131 us (0.910)
  the two profiles are of different devices: /device:TPU:89 before, /device:TPU:15 now
where the time goes in v2:
time: 131 us; the launch traced here: 130 us
  Pallas kernels  128 us (98%)
  other arithmetic  2.1 us (2%)
    pallas_call x1, Pallas kernels, on_device(): pl.pallas_call(kernel, out_shape=(out, out), in_specs=[vmem, vmem, pl.Blo...  128 us

profile of v2, /device:TPU:15, one launch (start us, length us, event | category | flops | bytes accessed | tf_op | source)
XLA Modules:
  0.0 130.5 jit_solution(6108260136397672494)
XLA Ops:
  0.6 127.7 %shard_map.77 = (bf16[64,2048]{1,0:T(8,128)(2,1)}, bf16[64,2048]{1,0:T(8,128)(2,1)}) custom-call(s32[64,128]{1,0:T(8,128)} %bitcast.10, s32[1,128]{1,0:T(1,128)} %bitcast.13, s32[32,32]{1,0:T(8,128)} %bands.1, f32[16,128]{1,0:T(8,128)} %bitcast.12, bf16[64,128]{1,0:T(8,128)(2,1)} %bitcast.11, bf16[64,2048]{1,0:T(8,128)(2,1)} %bitcast.9), custom_call_target="tpu_custom_call" | custom-call | tf_op jit(solution)/shard_map/pallas_call | solution.py:311
  128.4 2.1 %convert_bitcast_fusion = (f32[2048,64]{0,1:T(8,128)}, f32[2048,64]{0,1:T(8,128)}) fusion(bf16[64,2048]{1,0:T(8,128)(2,1)} %get-tuple-element.5, bf16[64,2048]{1,0:T(8,128)(2,1)} %get-tuple-element.4), kind=kLoop, calls=%fused_computation | loop fusion | flops 262144 | bytes 1572864 | tf_op jit(solution)/shard_map/convert_element_type | solution.py:351

commit v3 on v2

v3 whole, which is shorter than its diff:
```python
import jax
import jax.numpy as jnp
from jax import lax
from jax.experimental import pallas as pl
from jax.experimental.pallas import tpu as pltpu
from jax.sharding import PartitionSpec as P

NZ, NH, NL, NX, NU = 8, 2, 4, 4, 2
NY = NH * NL
ROWS = 128
HALF = ROWS // 2
SUBAP = 2048
SHARDS = NY * NX * NU
PIECES = NZ
TILE = NU * ROWS
TILES = SHARDS // NU
TILES_SENSOR = SUBAP // TILE
SLOTS = 16
CHUNK = 4
MESH = pl.DeviceIdType.MESH
damping = 0.4
f32, bf16 = jnp.float32, jnp.bfloat16


def kernel(
    telemetry, scales, bands, noise, start, target, out1, out2,
    joined, colb, rowp, srow, inv, cov, dist, acc, bsend, brecv, dsend, drecv,
    tgt, noises, noi, low1, low2, cbuf, zbuf1, zbuf2, ebuf1, ebuf2,
    send_a, recv_a, send_r, recv_r, send_t, recv_t, send_n, recv_n, send_b, recv_b,
    send_c, recv_c, send_d, recv_d, send_g, recv_g, send_h, recv_h, send_e, recv_e, send_f, recv_f,
):
    row, col = lax.axis_index("row"), lax.axis_index("col")
    z, h = col // NH, col % NH
    l, x, u = row // (NX * NU), row // NU % NX, row % NU
    y = h * NL + l

    def rowid(yy, xx, uu):
        return yy % NL * (NX * NU) + xx * NU + uu

    def colid(zz, yy):
        return zz * NH + yy // NL

    def at(zz, yy, xx, uu):
        return rowid(yy, xx, uu), colid(zz, yy)

    def shard(yy, xx, uu):
        return (yy * NX + xx) * NU + uu

    def remote(src, dst, ssem, rsem, dev):
        return pltpu.make_async_remote_copy(
            src_ref=src, dst_ref=dst, send_sem=ssem, recv_sem=rsem, device_id=dev, device_id_type=MESH
        )

    def put_maybe_self(src, dst, ssem, rsem, dev):
        mine = (dev[0] == row) & (dev[1] == col)

        @pl.when(mine)
        def _():
            pltpu.make_async_copy(src, dst, rsem).start()

        @pl.when(jnp.logical_not(mine))
        def _():
            remote(src, dst, ssem, rsem, dev).start()

    me = shard(y, x, u)
    here = (row, col)
    xl, xr, xo = (x + NX - 1) % NX, (x + 1) % NX, (x + 2) % NX

    def near(i, start, size):
        return (start + i % 2 * ((i + 1) // 2) - (1 - i % 2) * (i // 2) + size) % size

    def y_of(i):
        return near(i, y, NY)

    def piece(i):
        return near(PIECES - 1 - i, z, NZ)

    zs = [near(i, z, NZ) for i in range(NZ - 1, 0, -1)]

    barrier = pltpu.get_barrier_semaphore()
    greet = [at(zz, y, x, u) for zz in zs] + [at(z, y_of(i), x, u) for i in range(1, NY)]
    greet += [at(z, y, xl, u), at(z, y, xr, u), at(z, y, x, 1 - u)]
    for dev in greet:
        pl.semaphore_signal(barrier, inc=1, device_id=dev, device_id_type=MESH)

    slopes = telemetry[...].astype(f32) * scales[...].astype(f32) * (1.0 / 128.0)
    joined[:HALF, :] = slopes.astype(bf16)
    joined[HALF:, :] = start[...]
    for s in range(SLOTS):
        noises[s] = jnp.broadcast_to(noise[s : s + 1, :], (8, ROWS))
    colb[me] = joined[...]
    rowp[z] = joined[:HALF, :]

    p0 = (l % 2 * (NX * NU) + x * NU + u) * ROWS
    base_d = (
        p0 + lax.broadcasted_iota(jnp.int32, (ROWS, TILE), 0) - lax.broadcasted_iota(jnp.int32, (ROWS, TILE), 1)
    )
    for t in range(TILES_SENSOR):
        dist[t] = jnp.abs(base_d - t * TILE).astype(f32)
    for i in range(PIECES):
        for k in range(NL):
            a, b = NL * piece(i) + y // 2, NL * z + k
            band = bands[jnp.minimum(a, b), jnp.maximum(a, b)].astype(f32)
            inv[i * NL + k] = 1.0 / jnp.full((1, TILE), band, f32)
    acc[...] = jnp.zeros_like(acc)
    pl.semaphore_wait(barrier, len(greet))

    left, right, other = at(z, y, xl, u), at(z, y, xr, u), at(z, y, x, 1 - u)

    def plane_gather(src, buf, ssem, rsem):
        def send(k, s_src, s, dev):
            remote(s_src, buf.at[s], ssem.at[k], rsem.at[s], dev).start()

        def wait(s):
            remote(src, buf.at[s], ssem.at[0], rsem.at[s], here).wait_recv()

        def begin():
            for i in range(NY - 1, 0, -1):
                send(i - 1, src, me, at(z, y_of(i), x, u))
            for k, dev in enumerate((left, right, other)):
                send(NY - 1 + k, src, me, dev)

        def y_step(i):
            s = shard(y_of(i), x, u)
            wait(s)
            for k, dev in enumerate((left, right, other)):
                send(NY - 1 + 3 * i + k, buf.at[s], s, dev)

        def x_step(i):
            yy = y_of(i)
            k = 4 * NY - 1 + 3 * i
            s = shard(yy, xl, u)
            wait(s)
            pl.when(yy % 2 == 0)(lambda s=s: send(k, buf.at[s], s, right))
            send(k + 1, buf.at[s], s, other)
            s = shard(yy, xr, u)
            wait(s)
            pl.when(yy % 2 == 1)(lambda s=s: send(k, buf.at[s], s, left))
            send(k + 2, buf.at[s], s, other)

        def o_step(i):
            s = shard(y_of(i), xo, u)
            wait(s)
            send(7 * NY - 1 + i, buf.at[s], s, other)

        def other_step(i):
            for xx in range(NX):
                wait(shard(y_of(i), xx, 1 - u))

        def paced(step):
            def relay(i, carry):
                pl.when(i < NY)(lambda: x_step(i))
                pl.when((i >= 1) & (i <= NY))(lambda: o_step(i - 1))

                @pl.when(i >= 2)
                def _():
                    other_step(i - 2)
                    step(i - 2)

                return carry

            lax.fori_loop(0, NY + 2, relay, 0)

        def drain():
            def one(k, carry):
                remote(src, buf.at[me], ssem.at[k], rsem.at[me], here).wait_send()
                return carry

            lax.fori_loop(0, 8 * NY - 1, one, 0)

        return begin, y_step, paced, drain

    mine_s = joined.at[pl.ds(0, HALF)]
    begin_a, y_step_a, paced_a, drain_a = plane_gather(joined, colb, send_a, recv_a)
    begin_a()
    for k, zz in enumerate(zs):
        remote(mine_s, rowp.at[z], send_r.at[k], recv_r.at[z], at(zz, y, x, u)).start()
    for i in range(1, NY):
        y_step_a(i)
    for zz in zs:
        remote(mine_s, rowp.at[zz], send_r.at[0], recv_r.at[zz], here).wait_recv()
    for i in range(PIECES):
        v = rowp[piece(i)].astype(f32) * (1.0 / 16384.0)
        srow[pl.ds(i * ROWS, ROWS), :] = jnp.transpose(v).astype(bf16)

    contract_last = (((1,), (1,)), ((), ()))
    slope_rows, panel_rows = slice(0, HALF), slice(HALF, ROWS)

    def wide(ref, t, part):
        return jnp.concatenate([ref[NU * t + i, part, :] for i in range(NX * NU)], axis=1)

    def rows_of(c):
        return pl.ds(c * CHUNK * ROWS, CHUNK * ROWS)

    def build(c, yy):
        span, t0 = rows_of(c), yy * NX
        entries = []
        for n in range(NX):
            cols = jnp.concatenate([colb[NU * (t0 + n) + i, slope_rows, :] for i in range(NU)], axis=1)
            raw = jnp.dot(srow[span, :], cols, preferred_element_type=f32)
            d = dist[yy % 2 * NX + n]
            parts = []
            for i in range(CHUNK):
                taper = jnp.maximum(0.0, 1.0 - d * inv[(c * CHUNK + i) * NL + yy // 2])
                parts.append((taper * raw[i * ROWS : (i + 1) * ROWS, :]).astype(bf16))
            entry = jnp.concatenate(parts, axis=0)
            cov[t0 + n, span, :] = entry
            entries.append(entry)
        acc[span, :] += lax.dot_general(
            jnp.concatenate(entries, axis=1), wide(colb, t0, panel_rows), contract_last, preferred_element_type=f32
        )

    def multiply(c, yy):
        span, t0 = rows_of(c), yy * NX
        entries = jnp.concatenate([cov[t0 + n, span, :] for n in range(NX)], axis=1)
        acc[span, :] += lax.dot_general(
            entries, wide(cbuf, t0, slice(None)), contract_last, preferred_element_type=f32
        )

    def send_rows(c, sbuf, rbuf, ssem, rsem):
        for i in range(c * CHUNK, (c + 1) * CHUNK):
            sbuf[i] = jnp.transpose(acc[pl.ds(i * ROWS, ROWS), :])
            if i < PIECES - 1:
                remote(sbuf.at[i], rbuf.at[z], ssem.at[i], rsem.at[z], at(piece(i), y, x, u)).start()

    def rest(c, step):
        def one(yy, carry):
            step(c, yy)
            return carry

        lax.fori_loop(0, NY, one, 0)

    paced_a(lambda i: build(0, y_of(i)))
    send_rows(0, bsend, brecv, send_b, recv_b)

    def target_part(slot):
        return target.at[:, pl.ds(pl.multiple_of(slot * ROWS, ROWS), ROWS)]

    source = (l == z // 2) & (x // 2 == z % 2)
    owner_dev = []
    for xx in range(NX):
        for uu in range(NU):
            slot = h * (NX * NU) + xx * NU + uu
            dev = ((2 * u + h) * (NX * NU) + xx * NU + uu, z * NH + x % NH)
            owner_dev.append((slot, dev))

    @pl.when(source)
    def _():
        for k, (slot, dev) in enumerate(owner_dev):
            put_maybe_self(target_part(slot), tgt, send_t.at[k], recv_t, dev)
            put_maybe_self(noises.at[slot], noi, send_n.at[k], recv_n, dev)

    for c in range(1, PIECES // CHUNK):
        rest(c, build)
        send_rows(c, bsend, brecv, send_b, recv_b)

    def collected(sbuf, rbuf, rsem):
        total = sbuf[PIECES - 1]
        for zz in zs:
            remote(sbuf.at[0], rbuf.at[zz], send_b.at[0], rsem.at[zz], here).wait_recv()
            total = total + rbuf[zz]
        return total

    remote(target_part(0), tgt, send_t.at[0], recv_t, here).wait_recv()
    remote(noises.at[0], noi, send_n.at[0], recv_n, here).wait_recv()
    s_own = joined[:HALF, :].astype(f32)
    x_own = joined[HALF:, :].astype(f32)
    raw_own = jnp.sum(s_own * s_own, axis=0, keepdims=True) * (1.0 / 16384.0)
    diag = raw_own + noi[0:1, :]
    weight = damping / diag
    extra = diag.astype(bf16).astype(f32) - raw_own.astype(bf16).astype(f32)
    tgt_own = tgt[...].astype(f32)

    first = x_own + weight * (tgt_own - (collected(bsend, brecv, recv_b) + extra * x_own))
    low1[...] = first.astype(bf16)

    slot_me = l % 2 * (NX * NU) + x * NU + u
    nearest = [near(i, z, NZ) for i in range(NZ)]

    def along_z(src, zbuf, ssem, rsem):
        for k, zz in enumerate(zs):
            remote(src, zbuf.at[z], ssem.at[k], rsem.at[z], at(zz, y, x, u)).start()
        zbuf[z] = src[...]

    def along_z_sent(src, zbuf, ssem, rsem):
        for k, zz in enumerate(zs):
            remote(src, zbuf.at[z], ssem.at[k], rsem.at[z], here).wait_send()

    def out_dev(zz, hh):
        return zz // 2 * (NX * NU) + (zz % 2 * 2 + h) * NU + l // 2, z * NH + hh

    def spread(src, zbuf, zsem, buf, ssem, rsem):
        for i, zz in enumerate(nearest):
            if i:
                remote(src, zbuf.at[zz], ssem.at[0], zsem.at[zz], here).wait_recv()
            for hh in range(NH):
                part = zbuf.at[zz] if i else src
                put_maybe_self(part, buf.at[slot_me], ssem.at[i * NH + hh], rsem.at[slot_me], out_dev(zz, hh))

    def spread_sent(src, buf, ssem, rsem):
        for i, zz in enumerate(nearest):
            for hh in range(NH):
                dev = out_dev(zz, hh)

                @pl.when(jnp.logical_not((dev[0] == row) & (dev[1] == col)))
                def _():
                    remote(src, buf.at[slot_me], ssem.at[i * NH + hh], rsem.at[slot_me], dev).wait_send()

    def unpack_out(src, buf, rsem, out):
        for s in range(SLOTS):
            remote(src, buf.at[s], send_e.at[0], rsem.at[s], here).wait_recv()
            out[:, pl.ds(s * ROWS, ROWS)] = buf[s]

    begin_c, y_step_c, paced_c, drain_c = plane_gather(low1, cbuf, send_c, recv_c)
    begin_c()
    along_z(low1, zbuf1, send_g, recv_g)
    cbuf[me] = low1[...]
    acc[...] = jnp.zeros_like(acc)
    for i in range(1, NY):
        y_step_c(i)
    paced_c(lambda i: multiply(0, y_of(i)))
    send_rows(0, dsend, drecv, send_d, recv_d)
    spread(low1, zbuf1, recv_g, ebuf1, send_e, recv_e)
    for c in range(1, PIECES // CHUNK):
        rest(c, multiply)
        send_rows(c, dsend, drecv, send_d, recv_d)

    product1 = collected(dsend, drecv, recv_d) + extra * first.astype(bf16).astype(f32)
    low2[...] = (first + weight * (tgt_own - product1)).astype(bf16)
    along_z(low2, zbuf2, send_h, recv_h)
    spread(low2, zbuf2, recv_h, ebuf2, send_f, recv_f)
    unpack_out(low1, ebuf1, recv_e, out1)
    unpack_out(low2, ebuf2, recv_f, out2)

    drain_a()
    drain_c()
    for k, zz in enumerate(zs):
        remote(mine_s, rowp.at[z], send_r.at[k], recv_r.at[z], at(zz, y, x, u)).wait_send()

    @pl.when(source)
    def _():
        for k, (slot, dev) in enumerate(owner_dev):
            @pl.when(jnp.logical_not((dev[0] == row) & (dev[1] == col)))
            def _():
                remote(target_part(slot), tgt, send_t.at[k], recv_t, dev).wait_send()
                remote(noises.at[slot], noi, send_n.at[k], recv_n, dev).wait_send()

    for i in range(PIECES - 1):
        remote(bsend.at[i], brecv.at[z], send_b.at[i], recv_b.at[z], here).wait_send()
        remote(dsend.at[i], drecv.at[z], send_d.at[i], recv_d.at[z], here).wait_send()

    along_z_sent(low1, zbuf1, send_g, recv_g)
    along_z_sent(low2, zbuf2, send_h, recv_h)
    spread_sent(low1, ebuf1, send_e, recv_e)
    spread_sent(low2, ebuf2, send_f, recv_f)


def on_device(telemetry, scales, bands, noise, start, target):
    vmem = pl.BlockSpec(memory_space=pltpu.VMEM)
    dma, gathers = pltpu.SemaphoreType.DMA, SHARDS
    out = jax.ShapeDtypeStruct(target.shape[::-1], bf16)
    part = (HALF, ROWS)
    first, second = pl.pallas_call(
        kernel,
        out_shape=(out, out),
        in_specs=[vmem, vmem, pl.BlockSpec(memory_space=pltpu.SMEM), vmem, vmem, vmem],
        out_specs=(vmem, vmem),
        scratch_shapes=[
            pltpu.VMEM((ROWS, ROWS), bf16),
            pltpu.VMEM((SHARDS, ROWS, ROWS), bf16),
            pltpu.VMEM((PIECES, *part), bf16),
            pltpu.VMEM((PIECES * ROWS, HALF), bf16),
            pltpu.VMEM((PIECES * NL, 1, TILE), f32),
            pltpu.VMEM((TILES, PIECES * ROWS, TILE), bf16),
            pltpu.VMEM((TILES_SENSOR, ROWS, TILE), f32),
            pltpu.VMEM((PIECES * ROWS, HALF), f32),
            pltpu.VMEM((PIECES, *part), f32),
            pltpu.VMEM((PIECES, *part), f32),
            pltpu.VMEM((PIECES, *part), f32),
            pltpu.VMEM((PIECES, *part), f32),
            pltpu.VMEM(part, bf16),
            pltpu.VMEM((SLOTS, 8, ROWS), f32),
            pltpu.VMEM((8, ROWS), f32),
            pltpu.VMEM(part, bf16),
            pltpu.VMEM(part, bf16),
            pltpu.VMEM((SHARDS, *part), bf16),
            pltpu.VMEM((NZ, *part), bf16),
            pltpu.VMEM((NZ, *part), bf16),
            pltpu.VMEM((SLOTS, *part), bf16),
            pltpu.VMEM((SLOTS, *part), bf16),
            dma((gathers,)), dma((SHARDS,)),
            dma((NZ,)), dma((NZ,)),
            dma((8,)), dma,
            dma((8,)), dma,
            dma((NZ,)), dma((NZ,)),
            dma((gathers,)), dma((SHARDS,)),
            dma((NZ,)), dma((NZ,)),
            dma((NZ,)), dma((NZ,)),
            dma((NZ,)), dma((NZ,)),
            dma((SLOTS,)), dma((SLOTS,)),
            dma((SLOTS,)), dma((SLOTS,)),
        ],
        compiler_params=pltpu.CompilerParams(
            collective_id=0, has_side_effects=True, vmem_limit_bytes=60 * 2**20
        ),
    )(telemetry.T, scales.reshape(1, ROWS), bands, noise.reshape(SLOTS, ROWS), start.T, target.T)
    return first.T.astype(f32), second.T.astype(f32)


def solution(mesh):
    placed = (P(("col", "row"), None), P(("col", "row")), P(), P("row"), P(("col", "row"), None), P("row", None))
    return jax.shard_map(
        on_device,
        mesh=mesh,
        in_specs=placed,
        out_specs=(P("row", None), P("row", None)),
        check_vma=False,
    )
```

time: 131 us -> 108 us (0.82)
  the two profiles are of different devices: /device:TPU:15 before, /device:TPU:18 now
where the time goes in v3:
time: 108 us
  Pallas kernels  105 us (97%)
  other arithmetic  2.1 us (2%)
    pallas_call x1, Pallas kernels, on_device(): pl.pallas_call(kernel, out_shape=(out, out), in_specs=[vmem, vmem, pl.Blo...  105 us

profile of v3, /device:TPU:18, one launch (start us, length us, event | category | flops | bytes accessed | tf_op | source)
XLA Modules:
  0.0 107.8 jit_solution(6048176432677709876)
XLA Ops:
  0.6 105.1 %shard_map.77 = (bf16[64,2048]{1,0:T(8,128)(2,1)}, bf16[64,2048]{1,0:T(8,128)(2,1)}) custom-call(s32[64,128]{1,0:T(8,128)} %bitcast.10, s32[1,128]{1,0:T(1,128)} %bitcast.13, s32[32,32]{1,0:T(8,128)} %bands.1, f32[16,128]{1,0:T(8,128)} %bitcast.12, bf16[64,128]{1,0:T(8,128)(2,1)} %bitcast.11, bf16[64,2048]{1,0:T(8,128)(2,1)} %bitcast.9), custom_call_target="tpu_custom_call" | custom-call | tf_op jit(solution)/shard_map/pallas_call | solution.py:363
  105.7 2.1 %convert_bitcast_fusion = (f32[2048,64]{0,1:T(8,128)}, f32[2048,64]{0,1:T(8,128)}) fusion(bf16[64,2048]{1,0:T(8,128)(2,1)} %get-tuple-element.5, bf16[64,2048]{1,0:T(8,128)(2,1)} %get-tuple-element.4), kind=kLoop, calls=%fused_computation | loop fusion | flops 262144 | bytes 1572864 | tf_op jit(solution)/shard_map/convert_element_type | solution.py:407

commit v4 on v3

--- a/solution.py
+++ b/solution.py
@@ -148,18 +148,22 @@
                 wait(shard(y_of(i), xx, 1 - u))
 
         def paced(step):
+            def across(i, carry):
+                x_step(i)
+                return carry
+
             def relay(i, carry):
-                pl.when(i < NY)(lambda: x_step(i))
-                pl.when((i >= 1) & (i <= NY))(lambda: o_step(i - 1))
-
-                @pl.when(i >= 2)
+                pl.when(i < NY)(lambda: o_step(i))
+
+                @pl.when(i >= 1)
                 def _():
-                    other_step(i - 2)
-                    step(i - 2)
+                    other_step(i - 1)
+                    step(i - 1)
 
                 return carry
 
-            lax.fori_loop(0, NY + 2, relay, 0)
+            lax.fori_loop(0, NY, across, 0)
+            lax.fori_loop(0, NY + 1, relay, 0)
 
         def drain():
             def one(k, carry):
@@ -363,7 +367,7 @@
     first, second = pl.pallas_call(
         kernel,
         out_shape=(out, out),
-        in_specs=[vmem, vmem, pl.BlockSpec(memory_space=pltpu.SMEM), vmem, vmem, vmem],
+        in_specs=[vmem, vmem, pl.BlockSpec(memory_space=pltpu.SMEM), vmem, vmem, pl.BlockSpec(memory_space=pl.ANY)],
         out_specs=(vmem, vmem),
         scratch_shapes=[
             pltpu.VMEM((ROWS, ROWS), bf16),

time: 108 us -> 94.2 us (0.87)
  the two profiles are of different devices: /device:TPU:18 before, /device:TPU:15 now
where the time goes in v4:
time: 94.2 us; the launch traced here: 92.7 us
  Pallas kernels  90 us (96%)
  other arithmetic  2.1 us (2%)
    pallas_call x1, Pallas kernels, on_device(): pl.pallas_call(kernel, out_shape=(out, out), in_specs=[vmem, vmem, pl.Blo...  90 us
    convert_element_type x1, other arithmetic, on_device(): return (first.T.astype(f32), second.T.astype(f32))  2.1 us

profile of v4, /device:TPU:15, one launch (start us, length us, event | category | flops | bytes accessed | tf_op | source)
XLA Modules:
  0.0 92.7 jit_solution(9069811348889491363)
XLA Ops:
  0.6 90.0 %shard_map.77 = (bf16[64,2048]{1,0:T(8,128)(2,1)}, bf16[64,2048]{1,0:T(8,128)(2,1)}) custom-call(s32[64,128]{1,0:T(8,128)} %bitcast.10, s32[1,128]{1,0:T(1,128)} %bitcast.13, s32[32,32]{1,0:T(8,128)} %bands.1, f32[16,128]{1,0:T(8,128)} %bitcast.12, bf16[64,128]{1,0:T(8,128)(2,1)} %bitcast.11, bf16[64,2048]{1,0:T(8,128)(2,1)} %bitcast.9), custom_call_target="tpu_custom_call" | custom-call | tf_op jit(solution)/shard_map/pallas_call | solution.py:367
  90.6 2.1 %convert_bitcast_fusion = (f32[2048,64]{0,1:T(8,128)}, f32[2048,64]{0,1:T(8,128)}) fusion(bf16[64,2048]{1,0:T(8,128)(2,1)} %get-tuple-element.5, bf16[64,2048]{1,0:T(8,128)(2,1)} %get-tuple-element.4), kind=kLoop, calls=%fused_computation | loop fusion | flops 262144 | bytes 1572864 | tf_op jit(solution)/shard_map/convert_element_type | solution.py:411

commit v5 on v3

--- a/solution.py
+++ b/solution.py
@@ -17,6 +17,7 @@
 TILES_SENSOR = SUBAP // TILE
 SLOTS = 16
 CHUNK = 4
+AHEAD = 3
 MESH = pl.DeviceIdType.MESH
 damping = 0.4
 f32, bf16 = jnp.float32, jnp.bfloat16
@@ -79,7 +80,7 @@
 
     barrier = pltpu.get_barrier_semaphore()
     greet = [at(zz, y, x, u) for zz in zs] + [at(z, y_of(i), x, u) for i in range(1, NY)]
-    greet += [at(z, y, xl, u), at(z, y, xr, u), at(z, y, x, 1 - u)]
+    greet += [at(z, y, xl, u), at(z, y, xr, u), at(z, y, xo, u), at(z, y, x, 1 - u)]
     for dev in greet:
         pl.semaphore_signal(barrier, inc=1, device_id=dev, device_id_type=MESH)
 
@@ -105,7 +106,8 @@
     acc[...] = jnp.zeros_like(acc)
     pl.semaphore_wait(barrier, len(greet))
 
-    left, right, other = at(z, y, xl, u), at(z, y, xr, u), at(z, y, x, 1 - u)
+    other = at(z, y, x, 1 - u)
+    across = [at(z, y, xo, u), at(z, y, xl, u), at(z, y, xr, u)]
 
     def plane_gather(src, buf, ssem, rsem):
         def send(k, s_src, s, dev):
@@ -114,34 +116,25 @@
         def wait(s):
             remote(src, buf.at[s], ssem.at[0], rsem.at[s], here).wait_recv()
 
-        def begin():
-            for i in range(NY - 1, 0, -1):
+        def begin(beside):
+            send(NY - 1 + len(across), src, me, other)
+            for i in range(1, NY):
                 send(i - 1, src, me, at(z, y_of(i), x, u))
-            for k, dev in enumerate((left, right, other)):
-                send(NY - 1 + k, src, me, dev)
+                if i <= len(across):
+                    send(NY - 2 + i, src, me, across[i - 1])
+                beside(i)
 
         def y_step(i):
             s = shard(y_of(i), x, u)
             wait(s)
-            for k, dev in enumerate((left, right, other)):
-                send(NY - 1 + 3 * i + k, buf.at[s], s, dev)
+            for k, dev in enumerate((*across, other)):
+                send(NY - 1 + NX * i + k, buf.at[s], s, dev)
 
         def x_step(i):
-            yy = y_of(i)
-            k = 4 * NY - 1 + 3 * i
-            s = shard(yy, xl, u)
-            wait(s)
-            pl.when(yy % 2 == 0)(lambda s=s: send(k, buf.at[s], s, right))
-            send(k + 1, buf.at[s], s, other)
-            s = shard(yy, xr, u)
-            wait(s)
-            pl.when(yy % 2 == 1)(lambda s=s: send(k, buf.at[s], s, left))
-            send(k + 2, buf.at[s], s, other)
-
-        def o_step(i):
-            s = shard(y_of(i), xo, u)
-            wait(s)
-            send(7 * NY - 1 + i, buf.at[s], s, other)
+            for k, xx in enumerate((xl, xr, xo)):
+                s = shard(y_of(i), xx, u)
+                wait(s)
+                send((1 + NX) * NY - 1 + (NX - 1) * i + k, buf.at[s], s, other)
 
         def other_step(i):
             for xx in range(NX):
@@ -150,16 +143,15 @@
         def paced(step):
             def relay(i, carry):
                 pl.when(i < NY)(lambda: x_step(i))
-                pl.when((i >= 1) & (i <= NY))(lambda: o_step(i - 1))
-
-                @pl.when(i >= 2)
+
+                @pl.when(i >= AHEAD)
                 def _():
-                    other_step(i - 2)
-                    step(i - 2)
+                    other_step(i - AHEAD)
+                    step(i - AHEAD)
 
                 return carry
 
-            lax.fori_loop(0, NY + 2, relay, 0)
+            lax.fori_loop(0, NY + AHEAD, relay, 0)
 
         def drain():
             def one(k, carry):
@@ -172,9 +164,7 @@
 
     mine_s = joined.at[pl.ds(0, HALF)]
     begin_a, y_step_a, paced_a, drain_a = plane_gather(joined, colb, send_a, recv_a)
-    begin_a()
-    for k, zz in enumerate(zs):
-        remote(mine_s, rowp.at[z], send_r.at[k], recv_r.at[z], at(zz, y, x, u)).start()
+    begin_a(lambda i: remote(mine_s, rowp.at[z], send_r.at[i], recv_r.at[z], at(near(i, z, NZ), y, x, u)).start())
     for i in range(1, NY):
         y_step_a(i)
     for zz in zs:
@@ -223,9 +213,9 @@
             if i < PIECES - 1:
                 remote(sbuf.at[i], rbuf.at[z], ssem.at[i], rsem.at[z], at(piece(i), y, x, u)).start()
 
-    def rest(c, step):
+    def rest(step):
         def one(yy, carry):
-            step(c, yy)
+            step(1, yy)
             return carry
 
         lax.fori_loop(0, NY, one, 0)
@@ -250,9 +240,8 @@
             put_maybe_self(target_part(slot), tgt, send_t.at[k], recv_t, dev)
             put_maybe_self(noises.at[slot], noi, send_n.at[k], recv_n, dev)
 
-    for c in range(1, PIECES // CHUNK):
-        rest(c, build)
-        send_rows(c, bsend, brecv, send_b, recv_b)
+    rest(build)
+    send_rows(1, bsend, brecv, send_b, recv_b)
 
     def collected(sbuf, rbuf, rsem):
         total = sbuf[PIECES - 1]
@@ -277,14 +266,12 @@
     slot_me = l % 2 * (NX * NU) + x * NU + u
     nearest = [near(i, z, NZ) for i in range(NZ)]
 
-    def along_z(src, zbuf, ssem, rsem):
-        for k, zz in enumerate(zs):
-            remote(src, zbuf.at[z], ssem.at[k], rsem.at[z], at(zz, y, x, u)).start()
-        zbuf[z] = src[...]
+    def along_z(src, zbuf, ssem, rsem, i):
+        remote(src, zbuf.at[z], ssem.at[i], rsem.at[z], at(near(i, z, NZ), y, x, u)).start()
 
     def along_z_sent(src, zbuf, ssem, rsem):
-        for k, zz in enumerate(zs):
-            remote(src, zbuf.at[z], ssem.at[k], rsem.at[z], here).wait_send()
+        for i in range(1, NZ):
+            remote(src, zbuf.at[z], ssem.at[i], rsem.at[z], here).wait_send()
 
     def out_dev(zz, hh):
         return zz // 2 * (NX * NU) + (zz % 2 * 2 + h) * NU + l // 2, z * NH + hh
@@ -312,8 +299,7 @@
             out[:, pl.ds(s * ROWS, ROWS)] = buf[s]
 
     begin_c, y_step_c, paced_c, drain_c = plane_gather(low1, cbuf, send_c, recv_c)
-    begin_c()
-    along_z(low1, zbuf1, send_g, recv_g)
+    begin_c(lambda i: along_z(low1, zbuf1, send_g, recv_g, i))
     cbuf[me] = low1[...]
     acc[...] = jnp.zeros_like(acc)
     for i in range(1, NY):
@@ -321,21 +307,21 @@
     paced_c(lambda i: multiply(0, y_of(i)))
     send_rows(0, dsend, drecv, send_d, recv_d)
     spread(low1, zbuf1, recv_g, ebuf1, send_e, recv_e)
-    for c in range(1, PIECES // CHUNK):
-        rest(c, multiply)
-        send_rows(c, dsend, drecv, send_d, recv_d)
+    rest(multiply)
+    send_rows(1, dsend, drecv, send_d, recv_d)
 
     product1 = collected(dsend, drecv, recv_d) + extra * first.astype(bf16).astype(f32)
     low2[...] = (first + weight * (tgt_own - product1)).astype(bf16)
-    along_z(low2, zbuf2, send_h, recv_h)
+    for i in range(NZ - 1, 0, -1):
+        along_z(low2, zbuf2, send_h, recv_h, i)
     spread(low2, zbuf2, recv_h, ebuf2, send_f, recv_f)
     unpack_out(low1, ebuf1, recv_e, out1)
     unpack_out(low2, ebuf2, recv_f, out2)
 
     drain_a()
     drain_c()
-    for k, zz in enumerate(zs):
-        remote(mine_s, rowp.at[z], send_r.at[k], recv_r.at[z], at(zz, y, x, u)).wait_send()
+    for i in range(1, NZ):
+        remote(mine_s, rowp.at[z], send_r.at[i], recv_r.at[z], here).wait_send()
 
     @pl.when(source)
     def _():
@@ -363,7 +349,7 @@
     first, second = pl.pallas_call(
         kernel,
         out_shape=(out, out),
-        in_specs=[vmem, vmem, pl.BlockSpec(memory_space=pltpu.SMEM), vmem, vmem, vmem],
+        in_specs=[vmem, vmem, pl.BlockSpec(memory_space=pltpu.SMEM), vmem, vmem, pl.BlockSpec(memory_space=pl.ANY)],
         out_specs=(vmem, vmem),
         scratch_shapes=[
             pltpu.VMEM((ROWS, ROWS), bf16),

time: 108 us -> 83.8 us (0.78)
  the two profiles are of different devices: /device:TPU:18 before, /device:TPU:15 now
where the time goes in v5:
time: 83.8 us; the launch traced here: 83.5 us
  Pallas kernels  80.8 us (96%)
  other arithmetic  2.1 us (3%)
    pallas_call x1, Pallas kernels, on_device(): pl.pallas_call(kernel, out_shape=(out, out), in_specs=[vmem, vmem, pl.Blo...  80.8 us
    convert_element_type x1, other arithmetic, on_device(): return (first.T.astype(f32), second.T.astype(f32))  2.1 us

profile of v5, /device:TPU:15, one launch (start us, length us, event | category | flops | bytes accessed | tf_op | source)
XLA Modules:
  0.0 83.5 jit_solution(3066172265033165335)
XLA Ops:
  0.6 80.8 %shard_map.77 = (bf16[64,2048]{1,0:T(8,128)(2,1)}, bf16[64,2048]{1,0:T(8,128)(2,1)}) custom-call(s32[64,128]{1,0:T(8,128)} %bitcast.10, s32[1,128]{1,0:T(1,128)} %bitcast.13, s32[32,32]{1,0:T(8,128)} %bands.1, f32[16,128]{1,0:T(8,128)} %bitcast.12, bf16[64,128]{1,0:T(8,128)(2,1)} %bitcast.11, bf16[64,2048]{1,0:T(8,128)(2,1)} %bitcast.9), custom_call_target="tpu_custom_call" | custom-call | tf_op jit(solution)/shard_map/pallas_call | solution.py:349
  81.4 2.1 %convert_bitcast_fusion = (f32[2048,64]{0,1:T(8,128)}, f32[2048,64]{0,1:T(8,128)}) fusion(bf16[64,2048]{1,0:T(8,128)(2,1)} %get-tuple-element.5, bf16[64,2048]{1,0:T(8,128)(2,1)} %get-tuple-element.4), kind=kLoop, calls=%fused_computation | loop fusion | flops 262144 | bytes 1572864 | tf_op jit(solution)/shard_map/convert_element_type | solution.py:393

commit v6 on v5

--- a/solution.py
+++ b/solution.py
@@ -24,8 +24,8 @@
 
 
 def kernel(
-    telemetry, scales, bands, noise, start, target, out1, out2,
-    joined, colb, rowp, srow, inv, cov, dist, acc, bsend, brecv, dsend, drecv,
+    telemetry_in, scales_in, bands_in, noise_in, start, target, out1, out2,
+    telemetry, scales, bands, noise, loaded, joined, colb, rowp, srow, inv, cov, dist, acc, bsend, brecv, dsend, drecv,
     tgt, noises, noi, low1, low2, cbuf, zbuf1, zbuf2, ebuf1, ebuf2,
     send_a, recv_a, send_r, recv_r, send_t, recv_t, send_n, recv_n, send_b, recv_b,
     send_c, recv_c, send_d, recv_d, send_g, recv_g, send_h, recv_h, send_e, recv_e, send_f, recv_f,
@@ -84,13 +84,20 @@
     for dev in greet:
         pl.semaphore_signal(barrier, inc=1, device_id=dev, device_id_type=MESH)
 
-    slopes = telemetry[...].astype(f32) * scales[...].astype(f32) * (1.0 / 128.0)
-    joined[:HALF, :] = slopes.astype(bf16)
-    joined[HALF:, :] = start[...]
-    for s in range(SLOTS):
-        noises[s] = jnp.broadcast_to(noise[s : s + 1, :], (8, ROWS))
-    colb[me] = joined[...]
-    rowp[z] = joined[:HALF, :]
+    loads = [
+        pltpu.make_async_copy(src, dst, loaded.at[k])
+        for k, (src, dst) in enumerate(
+            (
+                (telemetry_in, telemetry),
+                (scales_in, scales),
+                (start, joined.at[pl.ds(HALF, HALF)]),
+                (bands_in, bands),
+                (noise_in, noise),
+            )
+        )
+    ]
+    for load in loads:
+        load.start()
 
     p0 = (l % 2 * (NX * NU) + x * NU + u) * ROWS
     base_d = (
@@ -98,12 +105,22 @@
     )
     for t in range(TILES_SENSOR):
         dist[t] = jnp.abs(base_d - t * TILE).astype(f32)
+    acc[...] = jnp.zeros_like(acc)
+    for load in loads:
+        load.wait()
+
+    slopes = telemetry[...].astype(f32) * scales[...].astype(f32) * (1.0 / 128.0)
+    joined[:HALF, :] = slopes.astype(bf16)
+    for s in range(SLOTS):
+        noises[s] = jnp.broadcast_to(noise[s : s + 1, :], (8, ROWS))
+    colb[me] = joined[...]
+    rowp[z] = joined[:HALF, :]
+
     for i in range(PIECES):
         for k in range(NL):
             a, b = NL * piece(i) + y // 2, NL * z + k
             band = bands[jnp.minimum(a, b), jnp.maximum(a, b)].astype(f32)
             inv[i * NL + k] = 1.0 / jnp.full((1, TILE), band, f32)
-    acc[...] = jnp.zeros_like(acc)
     pl.semaphore_wait(barrier, len(greet))
 
     other = at(z, y, x, 1 - u)
@@ -312,7 +329,7 @@
 
     product1 = collected(dsend, drecv, recv_d) + extra * first.astype(bf16).astype(f32)
     low2[...] = (first + weight * (tgt_own - product1)).astype(bf16)
-    for i in range(NZ - 1, 0, -1):
+    for i in range(1, NZ):
         along_z(low2, zbuf2, send_h, recv_h, i)
     spread(low2, zbuf2, recv_h, ebuf2, send_f, recv_f)
     unpack_out(low1, ebuf1, recv_e, out1)
@@ -349,9 +366,14 @@
     first, second = pl.pallas_call(
         kernel,
         out_shape=(out, out),
-        in_specs=[vmem, vmem, pl.BlockSpec(memory_space=pltpu.SMEM), vmem, vmem, pl.BlockSpec(memory_space=pl.ANY)],
+        in_specs=[pl.BlockSpec(memory_space=pltpu.HBM)] * 6,
         out_specs=(vmem, vmem),
         scratch_shapes=[
+            pltpu.VMEM(part, jnp.int32),
+            pltpu.VMEM((1, ROWS), jnp.int32),
+            pltpu.SMEM(bands.shape, jnp.int32),
+            pltpu.VMEM((SLOTS, ROWS), f32),
+            dma((5,)),
             pltpu.VMEM((ROWS, ROWS), bf16),
             pltpu.VMEM((SHARDS, ROWS, ROWS), bf16),
             pltpu.VMEM((PIECES, *part), bf16),
@@ -387,9 +409,11 @@
             dma((SLOTS,)), dma((SLOTS,)),
         ],
         compiler_params=pltpu.CompilerParams(
-            collective_id=0, has_side_effects=True, vmem_limit_bytes=60 * 2**20
+            collective_id=0, has_side_effects=True, vmem_limit_bytes=40 * 2**20
         ),
-    )(telemetry.T, scales.reshape(1, ROWS), bands, noise.reshape(SLOTS, ROWS), start.T, target.T)
+    )(*[pltpu.with_memory_space_constraint(a, pltpu.HBM) for a in (
+        telemetry.T, scales.reshape(1, ROWS), bands, noise.reshape(SLOTS, ROWS), start.T, target.T
+    )])
     return first.T.astype(f32), second.T.astype(f32)
 
 

time: 83.8 us -> 81.2 us (0.969)
  the two profiles are of different devices: /device:TPU:15 before, /device:TPU:16 now
where the time goes in v6:
time: 81.2 us; the launch traced here: 81 us
  Pallas kernels  79.3 us (98%)
  other arithmetic  1.07 us (1%)
    pallas_call x1, Pallas kernels, on_device(): pl.pallas_call(kernel, out_shape=(out, out), in_specs=[pl.BlockSpec(memor...  79.3 us

profile of v6, /device:TPU:16, one launch (start us, length us, event | category | flops | bytes accessed | tf_op | source)
XLA Modules:
  0.0 81.0 jit_solution(13348013572456602540)
XLA Ops:
  0.6 79.3 %shard_map.77 = (bf16[64,2048]{1,0:T(8,128)(2,1)S(1)}, bf16[64,2048]{1,0:T(8,128)(2,1)S(1)}) custom-call(s32[64,128]{1,0:T(8,128)} %bitcast.10, s32[1,128]{1,0:T(1,128)} %bitcast.13, s32[32,32]{1,0:T(8,128)} %bands_in.1, f32[16,128]{1,0:T(8,128)} %bitcast.12, bf16[64,128]{1,0:T(8,128)(2,1)} %bitcast.11, bf16[64,2048]{1,0:T(8,128)(2,1)} %bitcast.9), custom_call_target="tpu_custom_call" | custom-call | tf_op jit(solution)/shard_map/pallas_call | solution.py:366
  79.9 1.1 %convert_bitcast_fusion = (f32[2048,64]{0,1:T(8,128)}, f32[2048,64]{0,1:T(8,128)}) fusion(bf16[64,2048]{1,0:T(8,128)(2,1)S(1)} %get-tuple-element.5, bf16[64,2048]{1,0:T(8,128)(2,1)S(1)} %get-tuple-element.4), kind=kLoop, calls=%fused_computation | loop fusion | flops 262144 | bytes 1572864 | tf_op jit(solution)/shard_map/convert_element_type | solution.py:417

commit v7 on v6

--- a/solution.py
+++ b/solution.py
@@ -17,7 +17,7 @@
 TILES_SENSOR = SUBAP // TILE
 SLOTS = 16
 CHUNK = 4
-AHEAD = 3
+AHEAD = 2
 MESH = pl.DeviceIdType.MESH
 damping = 0.4
 f32, bf16 = jnp.float32, jnp.bfloat16
@@ -161,14 +161,11 @@
             def relay(i, carry):
                 pl.when(i < NY)(lambda: x_step(i))
 
-                @pl.when(i >= AHEAD)
-                def _():
-                    other_step(i - AHEAD)
-                    step(i - AHEAD)
-
+                other_step(i - AHEAD)
+                step(i - AHEAD)
                 return carry
 
-            lax.fori_loop(0, NY + AHEAD, relay, 0)
+            lax.fori_loop(AHEAD, NY + AHEAD, relay, 0)
 
         def drain():
             def one(k, carry):
@@ -177,13 +174,20 @@
 
             lax.fori_loop(0, 8 * NY - 1, one, 0)
 
-        return begin, y_step, paced, drain
+        def ahead():
+            for i in range(1, NY - 1):
+                y_step(i)
+            x_step(0)
+            y_step(NY - 1)
+            for i in range(1, AHEAD):
+                x_step(i)
+
+        return begin, ahead, paced, drain
 
     mine_s = joined.at[pl.ds(0, HALF)]
-    begin_a, y_step_a, paced_a, drain_a = plane_gather(joined, colb, send_a, recv_a)
+    begin_a, ahead_a, paced_a, drain_a = plane_gather(joined, colb, send_a, recv_a)
     begin_a(lambda i: remote(mine_s, rowp.at[z], send_r.at[i], recv_r.at[z], at(near(i, z, NZ), y, x, u)).start())
-    for i in range(1, NY):
-        y_step_a(i)
+    ahead_a()
     for zz in zs:
         remote(mine_s, rowp.at[zz], send_r.at[0], recv_r.at[zz], here).wait_recv()
     for i in range(PIECES):
@@ -315,12 +319,11 @@
             remote(src, buf.at[s], send_e.at[0], rsem.at[s], here).wait_recv()
             out[:, pl.ds(s * ROWS, ROWS)] = buf[s]
 
-    begin_c, y_step_c, paced_c, drain_c = plane_gather(low1, cbuf, send_c, recv_c)
+    begin_c, ahead_c, paced_c, drain_c = plane_gather(low1, cbuf, send_c, recv_c)
     begin_c(lambda i: along_z(low1, zbuf1, send_g, recv_g, i))
     cbuf[me] = low1[...]
     acc[...] = jnp.zeros_like(acc)
-    for i in range(1, NY):
-        y_step_c(i)
+    ahead_c()
     paced_c(lambda i: multiply(0, y_of(i)))
     send_rows(0, dsend, drecv, send_d, recv_d)
     spread(low1, zbuf1, recv_g, ebuf1, send_e, recv_e)

time: 81.2 us -> 80.4 us (level)
  Pallas kernels: 79.3 us -> 78.4 us
    pallas_call x1, Pallas kernels: 79.3 us -> 78.4 us  [on_device(): pl.pallas_call(kernel, out_shape=(out, out), in_specs=[pl.BlockSpec(memor...]
where the time goes in v7:
time: 80.4 us; the launch traced here: 80.2 us
  Pallas kernels  78.4 us (98%)
  other arithmetic  1.07 us (1%)
    pallas_call x1, Pallas kernels, on_device(): pl.pallas_call(kernel, out_shape=(out, out), in_specs=[pl.BlockSpec(memor...  78.4 us

profile of v7, /device:TPU:16, one launch (start us, length us, event | category | flops | bytes accessed | tf_op | source)
XLA Modules:
  0.0 80.2 jit_solution(17050413147184064620)
XLA Ops:
  0.6 78.4 %shard_map.77 = (bf16[64,2048]{1,0:T(8,128)(2,1)S(1)}, bf16[64,2048]{1,0:T(8,128)(2,1)S(1)}) custom-call(s32[64,128]{1,0:T(8,128)} %bitcast.10, s32[1,128]{1,0:T(1,128)} %bitcast.13, s32[32,32]{1,0:T(8,128)} %bands_in.1, f32[16,128]{1,0:T(8,128)} %bitcast.12, bf16[64,128]{1,0:T(8,128)(2,1)} %bitcast.11, bf16[64,2048]{1,0:T(8,128)(2,1)} %bitcast.9), custom_call_target="tpu_custom_call" | custom-call | tf_op jit(solution)/shard_map/pallas_call | solution.py:369
  79.1 1.1 %convert_bitcast_fusion = (f32[2048,64]{0,1:T(8,128)}, f32[2048,64]{0,1:T(8,128)}) fusion(bf16[64,2048]{1,0:T(8,128)(2,1)S(1)} %get-tuple-element.5, bf16[64,2048]{1,0:T(8,128)(2,1)S(1)} %get-tuple-element.4), kind=kLoop, calls=%fused_computation | loop fusion | flops 262144 | bytes 1572864 | tf_op jit(solution)/shard_map/convert_element_type | solution.py:420

commit v8 on v7

--- a/solution.py
+++ b/solution.py
@@ -320,10 +320,12 @@
             out[:, pl.ds(s * ROWS, ROWS)] = buf[s]
 
     begin_c, ahead_c, paced_c, drain_c = plane_gather(low1, cbuf, send_c, recv_c)
-    begin_c(lambda i: along_z(low1, zbuf1, send_g, recv_g, i))
+    begin_c(lambda i: None)
     cbuf[me] = low1[...]
     acc[...] = jnp.zeros_like(acc)
     ahead_c()
+    for i in range(1, NZ):
+        along_z(low1, zbuf1, send_g, recv_g, i)
     paced_c(lambda i: multiply(0, y_of(i)))
     send_rows(0, dsend, drecv, send_d, recv_d)
     spread(low1, zbuf1, recv_g, ebuf1, send_e, recv_e)

time: 80.4 us -> 80.1 us (level)
  the two profiles are of different devices: /device:TPU:16 before, /device:TPU:10 now
where the time goes in v8:
time: 80.1 us; the launch traced here: 79.9 us
  Pallas kernels  78.2 us (98%)
  other arithmetic  1.07 us (1%)
    pallas_call x1, Pallas kernels, on_device(): pl.pallas_call(kernel, out_shape=(out, out), in_specs=[pl.BlockSpec(memor...  78.2 us

profile of v8, /device:TPU:10, one launch (start us, length us, event | category | flops | bytes accessed | tf_op | source)
XLA Modules:
  0.0 79.9 jit_solution(10448221275521824171)
XLA Ops:
  0.6 78.2 %shard_map.77 = (bf16[64,2048]{1,0:T(8,128)(2,1)S(1)}, bf16[64,2048]{1,0:T(8,128)(2,1)S(1)}) custom-call(s32[64,128]{1,0:T(8,128)} %bitcast.10, s32[1,128]{1,0:T(1,128)} %bitcast.13, s32[32,32]{1,0:T(8,128)} %bands_in.1, f32[16,128]{1,0:T(8,128)} %bitcast.12, bf16[64,128]{1,0:T(8,128)(2,1)} %bitcast.11, bf16[64,2048]{1,0:T(8,128)(2,1)} %bitcast.9), custom_call_target="tpu_custom_call" | custom-call | tf_op jit(solution)/shard_map/pallas_call | solution.py:371
  78.8 1.1 %convert_bitcast_fusion = (f32[2048,64]{0,1:T(8,128)}, f32[2048,64]{0,1:T(8,128)}) fusion(bf16[64,2048]{1,0:T(8,128)(2,1)S(1)} %get-tuple-element.5, bf16[64,2048]{1,0:T(8,128)(2,1)S(1)} %get-tuple-element.4), kind=kLoop, calls=%fused_computation | loop fusion | flops 262144 | bytes 1572864 | tf_op jit(solution)/shard_map/convert_element_type | solution.py:422
